TPU v7x, 32 devices: a whole 2x2x4 slice. The times are simulated.
32 devices in a mesh: front: 4 (over z), row: 4 (over x, core), col: 2 (over y).
Axes of the slice: x: 2, y: 2, z: 4, core: 2. Of those that a mesh axis runs over, the one named last changes fastest.
Arguments:
- own_rows: float32 [4, 1536, 4096], P('front', 'row', 'col'), may hold values from -1.5 to 1.5
- child_rows: float32 [8192, 4096], P(('front', 'row'), 'col'), may hold values from -3 to 3
- child_dest: int32 [8192, 1], P(('front', 'row')), may hold values from 0 to 3; in each aligned block of 512 rows (0 to 511, 512 to 1023, ...) at most 256 rows name the same one
- child_stair: int32 [8192], P(('front', 'row')), may hold values from 0 to 7
Outputs:
- r_factor: float32 [4, 1024, 4096], P('front', 'row', 'col')
Inputs may be any that keep to these rules, and one draw needn't show every extreme that they name: `child_dest`: among the 512 rows of one device at most 256 name one parent, and in every draw some device has exactly 256 rows for some parent.
All inputs are finite; a program needn't handle non-finite values.
Results may differ from a plain program's by a relative error of at most 0.0003.
Values sent between devices are 32-bit elements; how exact they have to be, the bound alone decides.
A program may use at most 128 MiB of HBM per device.

v0:
```python
import jax
import jax.numpy as jnp
from jax import lax
from jax.experimental import pallas as pl
from jax.experimental.pallas import tpu as pltpu
from jax.sharding import PartitionSpec as P

PANEL_COLUMNS = 512
PANEL_COUNT = 2
STAIR_BLK = 128
BLOCK = 128
HALF = 64
TILE = 256
HI = lax.Precision.HIGHEST
TN = (((0,), (0,)), ((), ()))
NN = (((1,), (0,)), ((), ()))


def mm(a, b, dims=NN):
    return lax.dot_general(a, b, dims, precision=HI, preferred_element_type=jnp.float32)


def split(x):
    hi = x.astype(jnp.bfloat16)
    return hi, (x - hi.astype(jnp.float32)).astype(jnp.bfloat16)


def dot3(a, b, dims):
    a_hi, a_lo = a
    b_hi, b_lo = b

    def dot(x, y):
        return lax.dot_general(x, y, dims, preferred_element_type=jnp.float32)

    return dot(a_lo, b_hi) + dot(a_hi, b_lo) + dot(a_hi, b_hi)


def packed_index(row, col):
    return col * (col + 1) // 2 + row


def gram_kernel(own_lhs, child_lhs, *refs):
    *rhs_refs, out, square, lhs_hi, lhs_lo = refs
    n_own = own_lhs.shape[1]
    eliminated = out.shape[1]
    tiles = eliminated // TILE

    @pl.when(pl.program_id(0) == 0)
    def _():
        for src, start in ((own_lhs, 0), (child_lhs, n_own)):
            rows = src.shape[1]
            hi, lo = split(src[0])
            lhs_hi[start : start + rows] = hi
            lhs_lo[start : start + rows] = lo

    half = len(rhs_refs) // 2
    own_rhs = jnp.concatenate([ref[0] for ref in rhs_refs[:half]], 1)
    child_rhs = jnp.concatenate([ref[0] for ref in rhs_refs[half:]], 1)
    rhs = split(jnp.concatenate([own_rhs, child_rhs], 0))

    def lhs(row):
        cols = slice(row * TILE, (row + 1) * TILE)
        return lhs_hi[:, cols], lhs_lo[:, cols]

    for row in range(tiles):
        out[0, row * TILE : (row + 1) * TILE, :] = dot3(lhs(row), rhs, TN)

    for col in range(tiles):

        @pl.when(pl.program_id(0) == col)
        def _():
            for row in range(col + 1):
                square[packed_index(row, col)] = dot3(lhs(row), lhs(col), TN)


def gram(own, child, eliminated, parts):
    n_col, own_rows, half_cols = own.shape
    child_rows = child.shape[1]
    widths = [(half_cols - (eliminated if c == 0 else 0)) // parts for c in range(n_col)]
    skips = [eliminated // widths[0]] + [0] * (n_col - 1)
    tiles = packed_index(0, eliminated // TILE)

    def pieces(rows):
        return [
            pl.BlockSpec((1, rows, widths[c]), lambda q, c=c: (c, 0, skips[c] + q))
            for c in range(n_col)
        ]

    return pl.pallas_call(
        gram_kernel,
        out_shape=(
            jax.ShapeDtypeStruct((parts, eliminated, sum(widths)), jnp.float32),
            jax.ShapeDtypeStruct((tiles, TILE, TILE), jnp.float32),
        ),
        grid=(parts,),
        in_specs=[
            pl.BlockSpec((1, own_rows, eliminated), lambda q: (0, 0, 0)),
            pl.BlockSpec((1, child_rows, eliminated), lambda q: (0, 0, 0)),
        ]
        + pieces(own_rows)
        + pieces(child_rows),
        out_specs=(
            pl.BlockSpec((1, eliminated, sum(widths)), lambda q: (q, 0, 0)),
            pl.BlockSpec((tiles, TILE, TILE), lambda q: (0, 0, 0)),
        ),
        scratch_shapes=[pltpu.VMEM((own_rows + child_rows, eliminated), jnp.bfloat16)] * 2,
        cost_estimate=pl.CostEstimate(
            flops=6 * (own_rows + child_rows) * eliminated * half_cols * n_col,
            bytes_accessed=4 * (own_rows + child_rows + eliminated) * half_cols * n_col,
            transcendentals=0,
        ),
    )(own, child, *([own] * n_col), *([child] * n_col))


def small_inverse(block):
    lanes = lax.broadcasted_iota(jnp.int32, (HALF, HALF), 1)
    rows = lax.broadcasted_iota(jnp.int32, (HALF, HALF), 0)
    eye = (lanes == rows).astype(jnp.float32)
    both = jnp.concatenate([block, eye], 1)
    count = HALF // 8
    groups = [both[g * 8 : (g + 1) * 8] for g in range(count)]
    sub = lax.broadcasted_iota(jnp.int32, (8, 2 * HALF), 0)

    def column_of(g, j):
        return jnp.broadcast_to(groups[g][:, j : j + 1], (8, 2 * HALF))

    def row_of(x, s):
        return jnp.broadcast_to(x[s : s + 1], x.shape)

    for home in range(count):
        first = home * 8
        below = [[column_of(g, first + s) for s in range(8)] for g in range(home + 1, count)]
        columns = [column_of(home, first + s) for s in range(8)]
        solved = forward = groups[home]
        pivots = columns[0]
        for s in range(8):
            column = columns[s]
            pivot = row_of(column, s)
            inverse = 1.0 / pivot
            pivots = jnp.where(sub == s, pivot, pivots)
            forward = jnp.where(
                sub > s, forward - column * (row_of(forward, s) * inverse), forward
            )
            scaled = row_of(solved, s) * inverse
            solved = jnp.where(sub == s, scaled, solved - column * scaled)
            for t in range(s + 1, 8):
                scaled = row_of(columns[t], s) * inverse
                columns[t] = jnp.where(sub == s, scaled, columns[t] - column * scaled)
        groups[home] = forward * lax.rsqrt(pivots)
        spread = [row_of(solved, s) for s in range(8)]
        for g in range(home + 1, count):
            terms = [below[g - home - 1][s] * spread[s] for s in range(8)]
            while len(terms) > 1:
                terms = [terms[i] + terms[i + 1] for i in range(0, len(terms), 2)]
            groups[g] = groups[g] - terms[0]
    return jnp.concatenate(groups, 0)[:, HALF:]


def inverse_kernel(blocks, out, upper, work):
    n = out.shape[0]
    count = n // BLOCK
    for col in range(n // TILE):
        for row in range(col + 1):
            work[row * TILE : (row + 1) * TILE, col * TILE : (col + 1) * TILE] = blocks[
                packed_index(row, col)
            ]
    lanes = lax.broadcasted_iota(jnp.int32, (BLOCK, n), 1)
    rows = lax.broadcasted_iota(jnp.int32, (BLOCK, n), 0)

    def outer(k, carry):
        r = pl.multiple_of(k * BLOCK, BLOCK)
        d = work[pl.ds(r, BLOCK), pl.ds(r, BLOCK)]
        first = small_inverse(d[:HALF, :HALF])
        r12 = mm(first, d[:HALF, HALF:])
        second = small_inverse(d[HALF:, HALF:] - mm(r12, r12, TN))
        corner = -mm(second, mm(r12, first, TN))
        whole = jnp.concatenate(
            [
                jnp.concatenate([first, jnp.zeros((HALF, HALF), jnp.float32)], 1),
                jnp.concatenate([corner, second], 1),
            ],
            0,
        )
        here = (lanes >= r) & (lanes < r + BLOCK)
        top = dot3(split(whole), split(work[pl.ds(r, BLOCK), :]), NN)
        upper[pl.ds(r, BLOCK), :] = jnp.where(lanes >= rows + r, top, 0.0)
        work[pl.ds(r, BLOCK), :] = top
        work[pl.ds(r, BLOCK), pl.ds(r, BLOCK)] = whole

        def inner(j, c):
            s = pl.multiple_of(j * BLOCK, BLOCK)
            left = split(work[pl.ds(r, BLOCK), pl.ds(s, BLOCK)])
            right = split(work[pl.ds(r, BLOCK), :])
            kept = jnp.where(here, 0.0, work[pl.ds(s, BLOCK), :])
            work[pl.ds(s, BLOCK), :] = kept - dot3(left, right, TN)
            return c

        lax.fori_loop(k + 1, count, inner, 0)
        return carry

    lax.fori_loop(0, count, outer, 0)

    def finish(k, carry):
        r = pl.multiple_of(k * BLOCK, BLOCK)
        out[pl.ds(r, BLOCK), :] = jnp.where(lanes <= rows + r, work[pl.ds(r, BLOCK), :], 0.0)
        return carry

    lax.fori_loop(0, count, finish, 0)


def cholesky_inverse(blocks, n):
    return pl.pallas_call(
        inverse_kernel,
        out_shape=(jax.ShapeDtypeStruct((n, n), jnp.float32),) * 2,
        in_specs=[pl.BlockSpec(memory_space=pltpu.VMEM)],
        out_specs=(pl.BlockSpec(memory_space=pltpu.VMEM),) * 2,
        scratch_shapes=[pltpu.VMEM((n, n), jnp.float32)],
        cost_estimate=pl.CostEstimate(
            flops=80 * n * n * n, bytes_accessed=8 * n * n, transcendentals=n
        ),
    )(blocks)


def exchange_own(rows, n_col, col_index):
    share = rows.shape[0] // n_col
    arrived = [lax.dynamic_slice_in_dim(rows, col_index * share, share, 0)]
    for shift in range(1, n_col):
        leaving = lax.dynamic_slice_in_dim(rows, (col_index + shift) % n_col * share, share, 0)
        arrived.append(
            lax.ppermute(leaving, "col", [(i, (i + shift) % n_col) for i in range(n_col)])
        )
    blocks = []
    for source in range(n_col):
        block = arrived[0]
        for shift in range(1, n_col):
            block = jnp.where((source + shift) % n_col == col_index, arrived[shift], block)
        blocks.append(block)
    return jnp.stack(blocks)


def assemble_kernel(col_ref, piece, out):
    out[...] = piece[0]


def assemble(factor, col_index, share):
    parts, rows, width = factor.shape
    halves = width // share

    def source(b, col_ref):
        first = col_ref[0] == 0
        part = jnp.where(first, b % parts, b // halves)
        return part, 0, jnp.where(first, b // parts, b % halves)

    return pl.pallas_call(
        assemble_kernel,
        out_shape=jax.ShapeDtypeStruct((rows, parts * width), jnp.float32),
        grid_spec=pltpu.PrefetchScalarGridSpec(
            num_scalar_prefetch=1,
            grid=(parts * halves,),
            in_specs=[pl.BlockSpec((1, rows, share), source)],
            out_specs=pl.BlockSpec((rows, share), lambda b, col_ref: (0, b)),
        ),
    )(col_index.reshape(1).astype(jnp.int32), factor)


def body(own_rows, child_rows, child_dest, child_stair):
    n_front = lax.axis_size("front")
    row_count = lax.axis_size("row")
    n_col = lax.axis_size("col")
    source_rows, half_cols = child_rows.shape
    capacity = max(2, 2 * source_rows // n_front)
    col_index = lax.axis_index("col")
    own = exchange_own(own_rows[0], n_col, col_index)
    global_cols = col_index * half_cols + lax.broadcasted_iota(
        jnp.int32, (source_rows, half_cols), 1
    )
    masked_rows = jnp.where(global_cols >= (child_stair * STAIR_BLK)[:, None], child_rows, 0.0)
    targets = child_dest[:, 0]
    onehot = (targets[:, None] == jnp.arange(n_front, dtype=jnp.int32)[None, :]).astype(jnp.int32)
    slot = jnp.sum((jnp.cumsum(onehot, axis=0) - onehot) * onehot, axis=1)
    eliminated = PANEL_COUNT * PANEL_COLUMNS
    parts = row_count * n_col
    sub_cap = capacity // n_col
    position = (slot % n_col) * (n_front * sub_cap) + targets * sub_cap + slot // n_col
    send_block = (
        jnp.zeros((n_front * capacity, half_cols), jnp.float32).at[position].set(masked_rows)
    )
    child = lax.all_to_all(send_block, ("col", "front"), split_axis=0, concat_axis=0, tiled=True)
    child = child.reshape(n_col, n_front * sub_cap, half_cols)
    products, square = gram(own, child, eliminated, parts)
    square = lax.psum(square, ("col", "row"))
    products, square = lax.optimization_barrier((products, square))
    mine = lax.psum_scatter(products, ("col", "row"), scatter_dimension=0, tiled=True)[0]
    inverse, upper = cholesky_inverse(square, eliminated)
    factor = jnp.dot(
        inverse, mine, precision=lax.Precision.HIGH, preferred_element_type=jnp.float32
    )
    share = eliminated // parts
    part = col_index * row_count + lax.axis_index("row")
    piece = lax.dynamic_slice_in_dim(upper, part * share, share, 1)
    width = half_cols // parts
    factor = jnp.concatenate([piece, factor], 1)
    blocks = [factor[:, c * width : (c + 1) * width] for c in range(n_col)]
    factor = jnp.stack(blocks).reshape(parts, eliminated // row_count, width)
    factor = lax.all_to_all(factor, ("col", "row"), split_axis=0, concat_axis=0, tiled=True)
    return assemble(factor, col_index, share)[None]


def solution(mesh):
    placed = (
        P("front", "row", "col"),
        P(("front", "row"), "col"),
        P(("front", "row"), None),
        P(("front", "row")),
    )
    return jax.shard_map(
        body, mesh=mesh, in_specs=placed, out_specs=P("front", "row", "col"), check_vma=False
    )
```

profile of v0, /device:TPU:23, one launch (start us, length us, event | category | flops | bytes accessed | tf_op | source)
XLA Modules:
  0.0 448.2 jit_solution(5868066937295135015)
XLA Ops:
  6.5 0.7 broadcast_multiply_fusion
  7.2 0.7 fusion.15
  7.9 1.2 reduce-window.6
  9.1 0.2 slice_reduce_fusion
  9.3 0.2 reduce-window.9
  9.5 0.1 add_bitcast_fusion
  9.6 0.7 fusion.14
  10.3 0.7 compare_select_fusion
  11.0 8.8 %scatter_custom_fusion = f32[1024,2048]{1,0:T(8,128)} fusion(s32[512]{0:T(512)S(1)} %bitcast.56, f32[512,2048]{1,0:T(8,128)} %param.5, f32[]{:T(128)} %constant.60.clone.1, s32[2048]{0:T(1024)S(1)} %iota_add_fusion, s32[512]{0:T(512)S(1)} %broadcast_multiply_fusion), kind=kCustom, calls=%fused_computation.1 | custom fusion | flops 2097152 | bytes 12594176 | tf_op jit(solution)/shard_map/scatter | solution.py:286
  19.8 0.0 copy-start
  19.8 5.8 %all-to-all-start = ((f32[8,128,2048]{2,1,0:T(8,128)}), f32[8,128,2048]{2,1,0:T(8,128)}, u32[]{:S(2)}, u32[]{:S(2)}) async-start(f32[8,128,2048]{2,1,0:T(8,128)} %bitcast.50), calls=%async_computation | async-start | bytes 16777216 | tf_op jit(solution)/shard_map/all_to_all | solution.py:288
  25.7 0.0 all-reduce.2.cloned.1.call-start
  25.7 0.0 copy-done
  25.7 1.3 dynamic-slice_bitcast_fusion
  26.9 0.3 collective-permute-start
  27.2 100.0 %collective-permute-done = f32[192,2048]{1,0:T(8,128)} collective-permute-done((f32[192,2048]{1,0:T(8,128)}, f32[192,2048]{1,0:T(8,128)}, u32[]{:S(2)}, u32[]{:S(2)}) %collective-permute-start) | collective-permute-done | bytes 1572896 | tf_op jit(solution)/shard_map/ppermute | solution.py:230
  127.2 1.6 fusion.9
  128.8 1.9 pad_maximum_fusion.own_lhs.refs_0_.refs_1_
  130.7 76.5 %all-to-all-done = f32[8,128,2048]{2,1,0:T(8,128)} async-done(((f32[8,128,2048]{2,1,0:T(8,128)}), f32[8,128,2048]{2,1,0:T(8,128)}, u32[]{:S(2)}, u32[]{:S(2)}) %all-to-all-start) | async-done | bytes 8388640 | tf_op jit(solution)/shard_map/all_to_all | solution.py:288
  207.2 30.8 %shard_map.46 = (f32[8,1024,384]{2,1,0:T(8,128)}, f32[10,256,256]{2,1,0:T(8,128)}) custom-call(f32[2,192,2048]{2,1,0:T(8,128)} %pad_maximum_fusion.own_lhs.refs_0_.refs_1_, f32[2,512,2048]{2,1,0:T(8,128)} %bitcast.11.child_lhs.refs_2_.refs_3_, f32[2,192,2048]{2,1,0:T(8,128)} %pad_maximum_fusion.own_lhs.refs_0_.refs_1_, ...), custom_call_target="tpu_custom_call" | custom-call | flops 17716740096 | bytes 28311552 | tf_op jit(solution)/shard_map/pallas_call | solution.py:89
  238.0 0.0 all-reduce.2.cloned.1.call-update
  238.0 0.3 reduce-scatter.2.cloned.1.call-start
  238.3 62.9 %all-reduce.2.cloned.1.call-done.blocks = f32[10,256,256]{2,1,0:T(8,128)} async-done(((f32[10,256,256]{2,1,0:T(8,128)}), f32[10,256,256]{2,1,0:T(8,128)}) %all-reduce.2.cloned.1.call-update) | async-done | bytes 2621456 | tf_op jit(solution)/shard_map/psum | solution.py:291
  301.2 0.0 reduce-scatter.2.cloned.1.call-update
  301.2 62.2 %shard_map.47 = (f32[1024,1024]{1,0:T(8,128)}, f32[1024,1024]{1,0:T(8,128)}) custom-call(f32[10,256,256]{2,1,0:T(8,128)} %all-reduce.2.cloned.1.call-done.blocks), custom_call_target="tpu_custom_call" | custom-call | flops 85899345920 | bytes 8388608 | tf_op jit(solution)/shard_map/pallas_call | solution.py:212
  363.5 1.1 constant_dynamic-slice_fusion
  364.6 32.4 %reduce-scatter.2.cloned.1.call-done = f32[1,1024,384]{2,1,0:T(8,128)} async-done(((f32[8,1024,384]{2,1,0:T(8,128)}), f32[1,1024,384]{2,1,0:T(8,128)}) %reduce-scatter.2.cloned.1.call-update) | async-done | bytes 1572880 | tf_op jit(solution)/shard_map/reduce_scatter | solution.py:293
  397.0 5.7 %fusion.7 = f32[1024,384]{1,0:T(8,128)S(1)} fusion(f32[1024,1024]{1,0:T(8,128)} %get-tuple-element.15, f32[1,1024,384]{2,1,0:T(8,128)} %reduce-scatter.2.cloned.1.call-done), kind=kOutput, calls=%fused_computation.10 | convolution fusion | flops 2415919104 | bytes 7340032 | tf_op jit(solution)/shard_map/dot_general | solution.py:295
  402.7 0.2 fusion.11
  402.8 0.1 pad_maximum_fusion.1
  403.0 29.0 %all_to_all.14.piece = f32[8,256,256]{2,1,0:T(8,128)} all-to-all(f32[8,256,256]{2,1,0:T(8,128)S(1)} %bitcast.51), channel_id=1, replica_groups=mesh['front'=4,'row'=4,'col'=2] {'col','row'}, dimensions={0} | all-to-all | bytes 4194304 | tf_op jit(solution)/shard_map/all_to_all | solution.py:305
  431.9 9.5 %shard_map.48 = f32[256,2048]{1,0:T(8,128)} custom-call(s32[1]{0:T(128)} %bitcast.col_ref, f32[8,256,256]{2,1,0:T(8,128)} %all_to_all.14.piece), custom_call_target="tpu_custom_call" | custom-call | tf_op jit(solution)/shard_map/pallas_call | solution.py:254
  (1 shorter events, 0.0 us)
Async XLA Ops:
  19.8 5.8 %copy-start = (f32[1,384,2048]{2,1,0:T(8,128)S(1)}, f32[1,384,2048]{2,1,0:T(8,128)}, u32[]{:S(2)}) copy-start(f32[1,384,2048]{2,1,0:T(8,128)} %param.4) | copy-start | bytes 9437188
  19.8 187.4 %all-to-all-start = ((f32[8,128,2048]{2,1,0:T(8,128)}), f32[8,128,2048]{2,1,0:T(8,128)}, u32[]{:S(2)}, u32[]{:S(2)}) async-start(f32[8,128,2048]{2,1,0:T(8,128)} %bitcast.50), calls=%async_computation | async-start | bytes 16777216 | tf_op jit(solution)/shard_map/all_to_all | solution.py:288
  25.7 275.5 %all-reduce.2.cloned.1.call-start = ((), (), s32[]{:S(2)}) async-start(), calls=%async_computation.3 | async-start | bytes 5242880 | tf_op jit(solution)/shard_map/psum | solution.py:291
  26.9 100.3 %collective-permute-start = (f32[192,2048]{1,0:T(8,128)}, f32[192,2048]{1,0:T(8,128)}, u32[]{:S(2)}, u32[]{:S(2)}) collective-permute-start(f32[192,2048]{1,0:T(8,128)} %dynamic-slice_bitcast_fusion), channel_id=1, source_target_pairs={{0,1},{1,0},{2,3},{3,2},{4,5},{5,4},{6,7},{7,6},{8,9},{9,8},{10,11... | collective-permute-start | bytes 4718600 | tf_op jit(solution)/shard_map/ppermute | solution.py:230
  238.0 158.9 %reduce-scatter.2.cloned.1.call-start = ((), (), s32[]{:S(2)}) async-start(), calls=%async_computation.4 | async-start | bytes 14155776 | tf_op jit(solution)/shard_map/reduce_scatter | solution.py:293
Sparse Core Ops, SparseCore 0:
  238.2 62.9 all-reduce.1
  304.7 92.2 reduce-scatter.1
where the time goes:
time: 452 us; the launch traced here: 448 us
  waiting for transfers between devices  272 us (60%)
  Pallas kernels  102 us (23%)
  blocking collectives  29 us (6%)
  other arithmetic  16.9 us (4%)
  between operations  13.5 us (3%)
  starting transfers between devices  6.36 us (1%)
  matrix products  5.68 us (1%)
    ppermute x1, waiting for transfers between devices, exchange_own(): lax.ppermute(leaving, 'col', [(i, (i + shift) % n_col) for i in range(n_c...  100 us
    all_to_all x1, waiting for transfers between devices, body(): lax.all_to_all(send_block, ('col', 'front'), split_axis=0, concat_axis=0,...  76.5 us
    psum x1, waiting for transfers between devices, body(): square = lax.psum(square, ('col', 'row'))  62.9 us
    pallas_call x1, Pallas kernels, cholesky_inverse(): pl.pallas_call(inverse_kernel, out_shape=(jax.ShapeDtypeStruct((n, n), jn...  62.2 us
    reduce_scatter x1, waiting for transfers between devices, body(): lax.psum_scatter(products, ('col', 'row'), scatter_dimension=0, tiled=True)  32.4 us
    pallas_call x1, Pallas kernels, gram(): pl.pallas_call(gram_kernel, out_shape=(jax.ShapeDtypeStruct((parts, elimi...  30.8 us
    all_to_all x1, blocking collectives, body(): lax.all_to_all(factor, ('col', 'row'), split_axis=0, concat_axis=0, tiled...  29 us
    pallas_call x1, Pallas kernels, assemble(): pl.pallas_call(assemble_kernel, out_shape=jax.ShapeDtypeStruct((rows, par...  9.47 us
  transfers between devices with their start and end apart: 4, of which 4 were waited for; matrix products, arithmetic and copies ran while one was open for 1% of the time, Pallas kernels for 14%

commit v1 on v0

v1 whole, which is shorter than its diff:
```python
import functools
import jax
import jax.numpy as jnp
from jax import lax
from jax.experimental import pallas as pl
from jax.experimental.pallas import tpu as pltpu
from jax.sharding import PartitionSpec as P

PANEL_COLUMNS = 512
PANEL_COUNT = 2
STAIR_BLK = 128
BLOCK = 128
HALF = 64
TILE = 256
PIECE = 64
HI = lax.Precision.HIGHEST
TN = (((0,), (0,)), ((), ()))
NN = (((1,), (0,)), ((), ()))
MESH = pl.DeviceIdType.MESH


def mm(a, b, dims=NN):
    return lax.dot_general(a, b, dims, precision=HI, preferred_element_type=jnp.float32)


def split(x):
    hi = x.astype(jnp.bfloat16)
    return hi, (x - hi.astype(jnp.float32)).astype(jnp.bfloat16)


def dot3(a, b, dims):
    a_hi, a_lo = a
    b_hi, b_lo = b

    def dot(x, y):
        return lax.dot_general(x, y, dims, preferred_element_type=jnp.float32)

    return dot(a_lo, b_hi) + dot(a_hi, b_lo) + dot(a_hi, b_hi)


def shift_order(n):
    return sorted(range(1, n), key=lambda s: (-min(s, n - s), s))


def square_tiles(eliminated, n_col):
    tiles = eliminated // TILE
    packed = [(i, k) for i in range(tiles) for k in range(i, tiles)]
    return [packed[c::n_col] for c in range(n_col)]


def pick(col, values):
    out = values[0]
    for c in range(1, len(values)):
        out = jnp.where(col == c, values[c], out)
    return out


def remote(src, dst, send_sem, recv_sem, device):
    return pltpu.make_async_remote_copy(
        src_ref=src,
        dst_ref=dst,
        send_sem=send_sem,
        recv_sem=recv_sem,
        device_id=device,
        device_id_type=MESH,
    )


def front_kernel(
    n_front, n_col, cap, own, send, prod, square,
    rows, pan, hi, lo, zs, zr, ys, yr, here_sem,
):
    f = lax.axis_index("front")
    c = lax.axis_index("col")
    n_own, width = own.shape
    eliminated = pan.shape[1]
    order = [0] + shift_order(n_front)
    piece = min(PIECE, cap)
    per = cap // piece
    first = n_own + cap
    count = (n_front - 1) * per

    barrier = pltpu.get_barrier_semaphore()
    for s in range(1, n_front):
        pl.semaphore_signal(
            barrier, inc=1, device_id={"front": (f + s) % n_front}, device_id_type=MESH
        )
    for s in range(1, n_col):
        pl.semaphore_signal(
            barrier, inc=1, device_id={"col": (c + s) % n_col}, device_id_type=MESH
        )

    local = [
        pltpu.make_async_copy(own, rows.at[pl.ds(0, n_own)], here_sem.at[0]),
        pltpu.make_async_copy(
            send.at[pl.ds(0, cap)], rows.at[pl.ds(n_own, cap)], here_sem.at[1]
        ),
    ]
    for copy in local:
        copy.start()
    pl.semaphore_wait(barrier, n_front - 1 + n_col - 1)

    def z_copy(j, target):
        return remote(
            send.at[pl.ds(pl.multiple_of(cap + j * piece, piece), piece)],
            rows.at[pl.ds(pl.multiple_of(first + j * piece, piece), piece)],
            zs.at[j],
            zr.at[j],
            {"front": target},
        )

    for j in range(count):
        z_copy(j, (f + order[1 + j // per]) % n_front).start()

    def y_copy(slot, start, size, other):
        return remote(
            rows.at[pl.ds(start, size), pl.ds(0, eliminated)],
            pan.at[pl.ds(start, size)],
            ys.at[slot, other],
            yr.at[slot],
            {"col": other},
        )

    prod[...] = jnp.zeros_like(prod)
    square[...] = jnp.zeros_like(square)
    lists = square_tiles(eliminated, n_col)

    def consume(slot, start, size):
        @pl.when(c == 0)
        def _():
            for other in range(1, n_col):
                y_copy(slot, start, size, other).start()
            h, l = split(rows[pl.ds(start, size), pl.ds(0, eliminated)])
            hi[pl.ds(0, size)] = h
            lo[pl.ds(0, size)] = l

        @pl.when(c > 0)
        def _():
            y_copy(slot, start, size, 1).wait_recv()
            h, l = split(pan[pl.ds(start, size)])
            hi[pl.ds(0, size)] = h
            lo[pl.ds(0, size)] = l

        def lhs(i):
            at = pl.ds(pl.multiple_of(i * TILE, TILE), TILE)
            return hi[pl.ds(0, size), at], lo[pl.ds(0, size), at]

        def column(n, carry):
            at = pl.ds(pl.multiple_of(n * TILE, TILE), TILE)
            rhs = split(rows[pl.ds(start, size), at])
            for i in range(eliminated // TILE):
                prod[pl.ds(i * TILE, TILE), at] += dot3(lhs(i), rhs, TN)
            return carry

        lax.fori_loop(0, width // TILE, column, 0)
        for j in range(len(lists[0])):
            a = pick(c, [t[min(j, len(t) - 1)][0] for t in lists])
            b = pick(c, [t[min(j, len(t) - 1)][1] for t in lists])
            square[j] += dot3(lhs(a), lhs(b), TN)

    local[0].wait()
    consume(0, 0, n_own)
    local[1].wait()
    consume(1, n_own, cap)

    def arrived(j, carry):
        z_copy(j, f).wait_recv()
        consume(2 + j, pl.multiple_of(first + j * piece, piece), piece)
        return carry

    lax.fori_loop(0, count, arrived, 0)

    @pl.when(c == 0)
    def _():
        for other in range(1, n_col):
            y_copy(0, 0, n_own, other).wait_send()
            y_copy(1, n_own, cap, other).wait_send()

            def sent(j, carry):
                start = pl.multiple_of(first + j * piece, piece)
                y_copy(2 + j, start, piece, other).wait_send()
                return carry

            lax.fori_loop(0, count, sent, 0)

    def left(j, carry):
        z_copy(j, f).wait_send()
        return carry

    lax.fori_loop(0, count, left, 0)


def front_gram(own, send, n_front, n_col, cap, eliminated):
    n_own, width = own.shape
    total = n_own + n_front * cap
    piece = min(PIECE, cap)
    count = (n_front - 1) * (cap // piece)
    slots = len(square_tiles(eliminated, n_col)[0])
    most = max(n_own, cap)
    return pl.pallas_call(
        functools.partial(front_kernel, n_front, n_col, cap),
        out_shape=(
            jax.ShapeDtypeStruct((eliminated, width), jnp.float32),
            jax.ShapeDtypeStruct((slots, TILE, TILE), jnp.float32),
        ),
        in_specs=[pl.BlockSpec(memory_space=pl.ANY)] * 2,
        out_specs=(pl.BlockSpec(memory_space=pltpu.VMEM),) * 2,
        scratch_shapes=[
            pltpu.VMEM((total, width), jnp.float32),
            pltpu.VMEM((total, eliminated), jnp.float32),
            pltpu.VMEM((most, eliminated), jnp.bfloat16),
            pltpu.VMEM((most, eliminated), jnp.bfloat16),
            pltpu.SemaphoreType.DMA((count,)),
            pltpu.SemaphoreType.DMA((count,)),
            pltpu.SemaphoreType.DMA((count + 2, n_col)),
            pltpu.SemaphoreType.DMA((count + 2,)),
            pltpu.SemaphoreType.DMA((2,)),
        ],
        compiler_params=pltpu.CompilerParams(
            collective_id=0, has_side_effects=True, vmem_limit_bytes=60 << 20
        ),
    )(own, send)


def small_inverse(block):
    lanes = lax.broadcasted_iota(jnp.int32, (HALF, HALF), 1)
    rows = lax.broadcasted_iota(jnp.int32, (HALF, HALF), 0)
    eye = (lanes == rows).astype(jnp.float32)
    both = jnp.concatenate([block, eye], 1)
    count = HALF // 8
    groups = [both[g * 8 : (g + 1) * 8] for g in range(count)]
    sub = lax.broadcasted_iota(jnp.int32, (8, 2 * HALF), 0)

    def column_of(g, j):
        return jnp.broadcast_to(groups[g][:, j : j + 1], (8, 2 * HALF))

    def row_of(x, s):
        return jnp.broadcast_to(x[s : s + 1], x.shape)

    for home in range(count):
        first = home * 8
        below = [[column_of(g, first + s) for s in range(8)] for g in range(home + 1, count)]
        columns = [column_of(home, first + s) for s in range(8)]
        solved = forward = groups[home]
        pivots = columns[0]
        for s in range(8):
            column = columns[s]
            pivot = row_of(column, s)
            inverse = 1.0 / pivot
            pivots = jnp.where(sub == s, pivot, pivots)
            forward = jnp.where(
                sub > s, forward - column * (row_of(forward, s) * inverse), forward
            )
            scaled = row_of(solved, s) * inverse
            solved = jnp.where(sub == s, scaled, solved - column * scaled)
            for t in range(s + 1, 8):
                scaled = row_of(columns[t], s) * inverse
                columns[t] = jnp.where(sub == s, scaled, columns[t] - column * scaled)
        groups[home] = forward * lax.rsqrt(pivots)
        spread = [row_of(solved, s) for s in range(8)]
        for g in range(home + 1, count):
            terms = [below[g - home - 1][s] * spread[s] for s in range(8)]
            while len(terms) > 1:
                terms = [terms[i] + terms[i + 1] for i in range(0, len(terms), 2)]
            groups[g] = groups[g] - terms[0]
    return jnp.concatenate(groups, 0)[:, HALF:]


def block_inverse(d):
    first = small_inverse(d[:HALF, :HALF])
    r12 = mm(first, d[:HALF, HALF:])
    second = small_inverse(d[HALF:, HALF:] - mm(r12, r12, TN))
    corner = -mm(second, mm(r12, first, TN))
    return jnp.concatenate(
        [
            jnp.concatenate([first, jnp.zeros((HALF, HALF), jnp.float32)], 1),
            jnp.concatenate([corner, second], 1),
        ],
        0,
    )


def tail_kernel(
    n_row, n_col, prod, square, out,
    part, other, whole_sq, work, near, leave, far, mine, ready,
    s1, s2, s3, s4, s5, r1, r2, ro_s, ro_r,
):
    r = lax.axis_index("row")
    c = lax.axis_index("col")
    eliminated, width = prod.shape
    share = width // n_row
    slots = square.shape[0]
    low = r % 2
    high = r // 2
    mate = r + 1 - 2 * low
    across = r + 2 - 4 * high
    y = n_col - 1 - c
    count = eliminated // BLOCK
    owner_rows = eliminated // n_row
    half = TILE // 2

    barrier = pltpu.get_barrier_semaphore()
    for s in range(1, n_row):
        pl.semaphore_signal(
            barrier, inc=1, device_id={"row": (r + s) % n_row}, device_id_type=MESH
        )
    pl.semaphore_signal(barrier, inc=1, device_id={"col": y}, device_id_type=MESH)
    pl.semaphore_wait(barrier, n_row)

    kept = pl.ds(pl.multiple_of(low * half, half), half)
    given = pl.ds(pl.multiple_of((1 - low) * half, half), half)

    def core_copy(j):
        return remote(square.at[j, given], part.at[j], s1.at[0, j], s1.at[1, j], {"row": mate})

    def x_copy(j):
        return remote(part.at[slots + j], other.at[j], s2.at[0, j], s2.at[1, j], {"row": across})

    def y_copy(j, col):
        tile = whole_sq.at[n_col * j + col, kept]
        return remote(tile, tile, s3.at[0, j], s3.at[1, j], {"col": y})

    def y_recv(j):
        tile = whole_sq.at[n_col * j + y, kept]
        return remote(tile, tile, s3.at[0, j], s3.at[1, j], {"col": y})

    def mate_copy(j, col, sems):
        tile = whole_sq.at[n_col * j + col, kept]
        return remote(tile, tile, sems.at[0, j], sems.at[1, j], {"row": mate})

    def mate_recv(j, col, sems):
        tile = whole_sq.at[n_col * j + col, given]
        return remote(tile, tile, sems.at[0, j], sems.at[1, j], {"row": mate})

    def near_copy(q):
        at = pl.ds(pl.multiple_of((2 * q + 1 - low) * share, share), share)
        return remote(prod.at[:, at], near.at[q], r1.at[0, q], r1.at[1, q], {"row": mate})

    def far_copy(k):
        at = pl.ds(pl.multiple_of(k * BLOCK, BLOCK), BLOCK)
        return remote(leave.at[at], far.at[at], r2.at[0, k], r2.at[1, k], {"row": across})

    for j in range(slots):
        core_copy(j).start()
    for q in range(n_row // 2):
        near_copy(q).start()
    for j in range(slots):
        core_copy(j).wait_recv()
        part[slots + j] = square[j, kept] + part[j]
        x_copy(j).start()
    for j in range(slots):
        x_copy(j).wait_recv()
        whole_sq[n_col * j + c, kept] = part[slots + j] + other[j]
        y_copy(j, c).start()
        mate_copy(j, c, s4).start()
    for q in range(n_row // 2):
        near_copy(q).wait_recv()

    def gather(k, carry):
        at = pl.ds(pl.multiple_of(k * BLOCK, BLOCK), BLOCK)
        theirs = pl.ds(pl.multiple_of((2 * (1 - high) + low) * share, share), share)
        ours = pl.ds(pl.multiple_of((2 * high + low) * share, share), share)
        leave[at] = prod[at, theirs] + near[1 - high, at]
        far_copy(k).start()
        mine[at] = prod[at, ours] + near[high, at]
        return carry

    lax.fori_loop(0, count, gather, 0)
    for j in range(slots):
        y_recv(j).wait_recv()
        mate_copy(j, y, s5).start()
    for j in range(slots):
        mate_recv(j, c, s4).wait_recv()
        mate_recv(j, y, s5).wait_recv()

    lists = square_tiles(eliminated, n_col)
    for col in range(n_col):
        for j, (a, b) in enumerate(lists[col]):
            work[a * TILE : (a + 1) * TILE, b * TILE : (b + 1) * TILE] = whole_sq[n_col * j + col]

    lanes = lax.broadcasted_iota(jnp.int32, (BLOCK, eliminated), 1)

    def result_copy(k):
        at = pl.ds(pl.multiple_of(k * BLOCK, BLOCK), BLOCK)
        owner = k * BLOCK // owner_rows
        inside = pl.ds(pl.multiple_of(k * BLOCK % owner_rows, BLOCK), BLOCK)
        cols = pl.ds(pl.multiple_of(r * share, share), share)
        return remote(
            ready.at[at],
            out.at[inside, cols],
            ro_s.at[k],
            ro_r.at[r, k % (owner_rows // BLOCK)],
            {"row": owner},
        )

    def result_recv(source, k):
        inside = pl.ds(k * BLOCK, BLOCK)
        cols = pl.ds(pl.multiple_of(source * share, share), share)
        return remote(
            ready.at[inside],
            out.at[inside, cols],
            ro_s.at[k],
            ro_r.at[source, k],
            {"row": source},
        )

    def outer(k, carry):
        r0 = pl.multiple_of(k * BLOCK, BLOCK)
        at = pl.ds(r0, BLOCK)
        whole = block_inverse(work[at, at])
        here = (lanes >= r0) & (lanes < r0 + BLOCK)
        top = dot3(split(whole), split(work[at, :]), NN)
        work[at, :] = top
        work[at, at] = whole

        def inner(j, carry):
            s0 = pl.multiple_of(j * BLOCK, BLOCK)
            to = pl.ds(s0, BLOCK)
            left = split(work[at, to])
            right = split(work[at, :])
            keep = jnp.where(here, 0.0, work[to, :])
            work[to, :] = keep - dot3(left, right, TN)
            return carry

        lax.fori_loop(k + 1, count, inner, 0)

        far_copy(k).wait_recv()
        mine[at] += far[at]

        def term(m, acc):
            to = pl.ds(pl.multiple_of(m * BLOCK, BLOCK), BLOCK)
            return acc + dot3(split(work[at, to]), split(mine[to]), NN)

        ready[at] = lax.fori_loop(0, k + 1, term, jnp.zeros((BLOCK, share), jnp.float32))
        owner = k * BLOCK // owner_rows

        @pl.when(owner == r)
        def _():
            inside = pl.ds(pl.multiple_of(k * BLOCK % owner_rows, BLOCK), BLOCK)
            out[inside, pl.ds(pl.multiple_of(r * share, share), share)] = ready[at]

        @pl.when(owner != r)
        def _():
            result_copy(k).start()

        return carry

    lax.fori_loop(0, count, outer, 0)

    for s in range(1, n_row):
        for k in range(owner_rows // BLOCK):
            result_recv((r + s) % n_row, k).wait_recv()

    def sent(k, carry):
        far_copy(k).wait_send()

        @pl.when(k * BLOCK // owner_rows != r)
        def _():
            result_copy(k).wait_send()

        return carry

    lax.fori_loop(0, count, sent, 0)
    for j in range(slots):
        core_copy(j).wait_send()
        x_copy(j).wait_send()
        y_copy(j, c).wait_send()
        mate_copy(j, c, s4).wait_send()
        mate_copy(j, y, s5).wait_send()
    for q in range(n_row // 2):
        near_copy(q).wait_send()


def tail(prod, square, n_row, n_col):
    eliminated, width = prod.shape
    share = width // n_row
    slots = square.shape[0]
    count = eliminated // BLOCK
    owner_rows = eliminated // n_row
    half = TILE // 2
    dma = pltpu.SemaphoreType.DMA
    return pl.pallas_call(
        functools.partial(tail_kernel, n_row, n_col),
        out_shape=jax.ShapeDtypeStruct((owner_rows, width), jnp.float32),
        in_specs=[pl.BlockSpec(memory_space=pltpu.VMEM)] * 2,
        out_specs=pl.BlockSpec(memory_space=pltpu.VMEM),
        scratch_shapes=[
            pltpu.VMEM((2 * slots, half, TILE), jnp.float32),
            pltpu.VMEM((slots, half, TILE), jnp.float32),
            pltpu.VMEM((n_col * slots, TILE, TILE), jnp.float32),
            pltpu.VMEM((eliminated, eliminated), jnp.float32),
            pltpu.VMEM((n_row // 2, eliminated, share), jnp.float32),
            pltpu.VMEM((eliminated, share), jnp.float32),
            pltpu.VMEM((eliminated, share), jnp.float32),
            pltpu.VMEM((eliminated, share), jnp.float32),
            pltpu.VMEM((eliminated, share), jnp.float32),
            dma((2, slots)),
            dma((2, slots)),
            dma((2, slots)),
            dma((2, slots)),
            dma((2, slots)),
            dma((2, n_row // 2)),
            dma((2, count)),
            dma((count,)),
            dma((n_row, owner_rows // BLOCK)),
        ],
        compiler_params=pltpu.CompilerParams(
            collective_id=1, has_side_effects=True, vmem_limit_bytes=60 << 20
        ),
    )(prod, square)


def body(own_rows, child_rows, child_dest, child_stair):
    n_front = lax.axis_size("front")
    n_row = lax.axis_size("row")
    n_col = lax.axis_size("col")
    source_rows, half_cols = child_rows.shape
    capacity = max(2, 2 * source_rows // n_front)
    col_index = lax.axis_index("col")
    global_cols = col_index * half_cols + lax.broadcasted_iota(
        jnp.int32, (source_rows, half_cols), 1
    )
    masked_rows = jnp.where(global_cols >= (child_stair * STAIR_BLK)[:, None], child_rows, 0.0)
    targets = child_dest[:, 0]
    onehot = (targets[:, None] == jnp.arange(n_front, dtype=jnp.int32)[None, :]).astype(jnp.int32)
    slot = jnp.sum((jnp.cumsum(onehot, axis=0) - onehot) * onehot, axis=1)
    shift = (targets - lax.axis_index("front")) % n_front
    rank = jnp.zeros_like(shift)
    for place, s in enumerate(shift_order(n_front)):
        rank = jnp.where(shift == s, place + 1, rank)
    position = rank * capacity + slot
    send = jnp.zeros((n_front * capacity, half_cols), jnp.float32).at[position].set(masked_rows)
    eliminated = PANEL_COUNT * PANEL_COLUMNS
    prod, square = front_gram(own_rows[0], send, n_front, n_col, capacity, eliminated)
    return tail(prod, square, n_row, n_col)[None]


def solution(mesh):
    placed = (
        P("front", "row", "col"),
        P(("front", "row"), "col"),
        P(("front", "row"), None),
        P(("front", "row")),
    )
    return jax.shard_map(
        body, mesh=mesh, in_specs=placed, out_specs=P("front", "row", "col"), check_vma=False
    )
```

time: 452 us -> 344 us (0.76)
  waiting for transfers between devices: 272 us -> 0 us
  Pallas kernels: 102 us -> 327 us
  blocking collectives: 29 us -> 0 us
  between operations: 13.5 us -> 0.02 us
  starting transfers between devices: 6.36 us -> 0 us
  matrix products: 5.68 us -> 0 us
    pallas_call x3 -> x2, Pallas kernels: 102 us -> 327 us  [the longest x1 221 us: front_gram(): pl.pallas_call(functools.partial(front_kernel, n_front, n_col, cap), out_...]
    ppermute x1 -> x0, waiting for transfers between devices: 100 us -> none  [exchange_own(): lax.ppermute(leaving, 'col', [(i, (i + shift) % n_col) for i in range(n_c...]
    all_to_all x1 -> x0, waiting for transfers between devices: 76.5 us -> none  [body(): lax.all_to_all(send_block, ('col', 'front'), split_axis=0, concat_axis=0,...]
    psum x1 -> x0, waiting for transfers between devices: 62.9 us -> none  [body(): square = lax.psum(square, ('col', 'row'))]
    reduce_scatter x1 -> x0, waiting for transfers between devices: 32.4 us -> none  [body(): lax.psum_scatter(products, ('col', 'row'), scatter_dimension=0, tiled=True)]
    all_to_all x1 -> x0, blocking collectives: 29 us -> none  [body(): lax.all_to_all(factor, ('col', 'row'), split_axis=0, concat_axis=0, tiled...]
    all_to_all x1 -> x0, starting transfers between devices: 5.81 us -> none  [body(): lax.all_to_all(send_block, ('col', 'front'), split_axis=0, concat_axis=0,...]
    dot_general x1 -> x0, matrix products: 5.68 us -> none  [body(): jnp.dot(inverse, mine, precision=lax.Precision.HIGH, preferred_element_ty...]
  transfers between devices with their start and end apart: 4 -> 0, of which waited for: 4 -> 0; matrix products, arithmetic and copies ran while one was open for 1% -> 0% of each run, Pallas kernels for 14% -> 0%
where the time goes in v1:
time: 344 us
  Pallas kernels  327 us (95%)
  other arithmetic  13.1 us (4%)
    pallas_call x1, Pallas kernels, front_gram(): pl.pallas_call(functools.partial(front_kernel, n_front, n_col, cap), out_...  221 us
    pallas_call x1, Pallas kernels, tail(): pl.pallas_call(functools.partial(tail_kernel, n_row, n_col), out_shape=ja...  106 us
    scatter x1, other arithmetic, body(): jnp.zeros((n_front * capacity, half_cols), jnp.float32).at[position]  8.82 us

profile of v1, /device:TPU:23, one launch (start us, length us, event | category | flops | bytes accessed | tf_op | source)
XLA Modules:
  0.0 343.5 jit_solution(8866623156612500440)
XLA Ops:
  0.0 0.7 broadcast_multiply_fusion
  0.7 0.7 fusion.10
  1.4 1.2 reduce-window.6
  2.6 0.2 slice_reduce_fusion
  2.8 0.2 reduce-window.9
  3.0 0.1 add_bitcast_fusion
  3.1 0.7 fusion.9
  3.8 0.7 compare_select_fusion
  4.5 8.8 %scatter_custom_fusion.send = f32[1024,2048]{1,0:T(8,128)} fusion(s32[512]{0:T(512)S(1)} %bitcast.32, f32[512,2048]{1,0:T(8,128)} %param.5, f32[]{:T(128)} %constant.14.clone.1, s32[2048]{0:T(1024)S(1)} %iota_add_fusion, s32[512]{0:T(512)S(1)} %broadcast_multiply_fusion), kind=kCustom, calls=%fused_computation.1 | custom fusion | flops 2097152 | bytes 12594176 | tf_op jit(solution)/shard_map/scatter | solution.py:532
  13.3 221.1 %shard_map.46 = (f32[1024,2048]{1,0:T(8,128)}, f32[5,256,256]{2,1,0:T(8,128)}) custom-call(f32[384,2048]{1,0:T(8,128)} %bitcast.27, f32[1024,2048]{1,0:T(8,128)} %scatter_custom_fusion.send), custom_call_target="tpu_custom_call" | custom-call | tf_op jit(solution)/shard_map/pallas_call | solution.py:200
  234.4 106.0 %shard_map.47 = f32[256,2048]{1,0:T(8,128)} custom-call(f32[1024,2048]{1,0:T(8,128)} %get-tuple-element.7.prod, f32[5,256,256]{2,1,0:T(8,128)} %get-tuple-element.8.square), custom_call_target="tpu_custom_call" | custom-call | tf_op jit(solution)/shard_map/pallas_call | solution.py:482
  340.4 3.1 copy.8
  (1 shorter events, 0.0 us)

commit v2 on v1

--- a/solution.py
+++ b/solution.py
@@ -13,14 +13,10 @@
 HALF = 64
 TILE = 256
 PIECE = 64
-HI = lax.Precision.HIGHEST
+CHUNK = 512
 TN = (((0,), (0,)), ((), ()))
 NN = (((1,), (0,)), ((), ()))
 MESH = pl.DeviceIdType.MESH
-
-
-def mm(a, b, dims=NN):
-    return lax.dot_general(a, b, dims, precision=HI, preferred_element_type=jnp.float32)
 
 
 def split(x):
@@ -112,6 +108,9 @@
     for j in range(count):
         z_copy(j, (f + order[1 + j // per]) % n_front).start()
 
+    groups = list(range(n_front - 1))
+    late = sorted(groups, key=lambda q: (-min(order[1 + q], n_front - order[1 + q]), -q))
+
     def y_copy(slot, start, size, other):
         return remote(
             rows.at[pl.ds(start, size), pl.ds(0, eliminated)],
@@ -163,7 +162,9 @@
     local[1].wait()
     consume(1, n_own, cap)
 
-    def arrived(j, carry):
+    def arrived(i, carry):
+        group = jnp.where(2 * f < n_front, i // per, pick(i // per, late))
+        j = group * per + i % per
         z_copy(j, f).wait_recv()
         consume(2 + j, pl.multiple_of(first + j * piece, piece), piece)
         return carry
@@ -242,10 +243,10 @@
         below = [[column_of(g, first + s) for s in range(8)] for g in range(home + 1, count)]
         columns = [column_of(home, first + s) for s in range(8)]
         solved = forward = groups[home]
-        pivots = columns[0]
+        pivot = row_of(columns[0], 0)
+        pivots = pivot
         for s in range(8):
             column = columns[s]
-            pivot = row_of(column, s)
             inverse = 1.0 / pivot
             pivots = jnp.where(sub == s, pivot, pivots)
             forward = jnp.where(
@@ -254,8 +255,11 @@
             scaled = row_of(solved, s) * inverse
             solved = jnp.where(sub == s, scaled, solved - column * scaled)
             for t in range(s + 1, 8):
-                scaled = row_of(columns[t], s) * inverse
-                columns[t] = jnp.where(sub == s, scaled, columns[t] - column * scaled)
+                row = row_of(columns[t], s)
+                fresh = columns[t] - (column * row) * inverse
+                if t == s + 1:
+                    pivot = row_of(fresh, t)
+                columns[t] = jnp.where(sub == s, row * inverse, fresh)
         groups[home] = forward * lax.rsqrt(pivots)
         spread = [row_of(solved, s) for s in range(8)]
         for g in range(home + 1, count):
@@ -268,9 +272,11 @@
 
 def block_inverse(d):
     first = small_inverse(d[:HALF, :HALF])
-    r12 = mm(first, d[:HALF, HALF:])
-    second = small_inverse(d[HALF:, HALF:] - mm(r12, r12, TN))
-    corner = -mm(second, mm(r12, first, TN))
+    first_parts = split(first)
+    r12 = dot3(first_parts, split(d[:HALF, HALF:]), NN)
+    r12_parts = split(r12)
+    second = small_inverse(d[HALF:, HALF:] - dot3(r12_parts, r12_parts, TN))
+    corner = -dot3(split(second), split(dot3(r12_parts, first_parts, TN)), NN)
     return jnp.concatenate(
         [
             jnp.concatenate([first, jnp.zeros((HALF, HALF), jnp.float32)], 1),
@@ -282,7 +288,8 @@
 
 def tail_kernel(
     n_row, n_col, prod, square, out,
-    part, other, whole_sq, work, near, leave, far, mine, ready,
+    part, other, whole_sq, work, near, leave, far, ready,
+    prev_hi, prev_lo,
     s1, s2, s3, s4, s5, r1, r2, ro_s, ro_r,
 ):
     r = lax.axis_index("row")
@@ -362,7 +369,7 @@
         ours = pl.ds(pl.multiple_of((2 * high + low) * share, share), share)
         leave[at] = prod[at, theirs] + near[1 - high, at]
         far_copy(k).start()
-        mine[at] = prod[at, ours] + near[high, at]
+        work[at, pl.ds(eliminated, share)] = prod[at, ours] + near[high, at]
         return carry
 
     lax.fori_loop(0, count, gather, 0)
@@ -377,8 +384,6 @@
     for col in range(n_col):
         for j, (a, b) in enumerate(lists[col]):
             work[a * TILE : (a + 1) * TILE, b * TILE : (b + 1) * TILE] = whole_sq[n_col * j + col]
-
-    lanes = lax.broadcasted_iota(jnp.int32, (BLOCK, eliminated), 1)
 
     def result_copy(k):
         at = pl.ds(pl.multiple_of(k * BLOCK, BLOCK), BLOCK)
@@ -404,34 +409,8 @@
             {"row": source},
         )
 
-    def outer(k, carry):
-        r0 = pl.multiple_of(k * BLOCK, BLOCK)
-        at = pl.ds(r0, BLOCK)
-        whole = block_inverse(work[at, at])
-        here = (lanes >= r0) & (lanes < r0 + BLOCK)
-        top = dot3(split(whole), split(work[at, :]), NN)
-        work[at, :] = top
-        work[at, at] = whole
-
-        def inner(j, carry):
-            s0 = pl.multiple_of(j * BLOCK, BLOCK)
-            to = pl.ds(s0, BLOCK)
-            left = split(work[at, to])
-            right = split(work[at, :])
-            keep = jnp.where(here, 0.0, work[to, :])
-            work[to, :] = keep - dot3(left, right, TN)
-            return carry
-
-        lax.fori_loop(k + 1, count, inner, 0)
-
-        far_copy(k).wait_recv()
-        mine[at] += far[at]
-
-        def term(m, acc):
-            to = pl.ds(pl.multiple_of(m * BLOCK, BLOCK), BLOCK)
-            return acc + dot3(split(work[at, to]), split(mine[to]), NN)
-
-        ready[at] = lax.fori_loop(0, k + 1, term, jnp.zeros((BLOCK, share), jnp.float32))
+    def deliver(k):
+        at = pl.ds(pl.multiple_of(k * BLOCK, BLOCK), BLOCK)
         owner = k * BLOCK // owner_rows
 
         @pl.when(owner == r)
@@ -443,6 +422,34 @@
         def _():
             result_copy(k).start()
 
+    lanes = lax.broadcasted_iota(jnp.int32, (BLOCK, eliminated), 1)
+    total = eliminated + share
+
+    def outer(k, carry):
+        at = pl.ds(pl.multiple_of(k * BLOCK, BLOCK), BLOCK)
+        scale = split(block_inverse(work[at, at]))
+        far_copy(k).wait_recv()
+        result = dot3(scale, split(work[at, eliminated:] + far[at]), NN)
+        ready[at] = result
+        prev_hi[:, eliminated:], prev_lo[:, eliminated:] = split(result)
+        top = dot3(scale, split(work[at, :eliminated]), NN)
+        top = jnp.where(lanes >= (k + 1) * BLOCK, top, 0.0)
+        prev_hi[:, :eliminated], prev_lo[:, :eliminated] = split(top)
+        deliver(k)
+
+        def inner(j, carry):
+            rows = pl.ds(pl.multiple_of(j * BLOCK, BLOCK), BLOCK)
+            left = prev_hi[:, rows], prev_lo[:, rows]
+            for start in range(0, total, CHUNK):
+                cols = slice(start, min(total, start + CHUNK))
+
+                @pl.when(j * BLOCK < cols.stop)
+                def _():
+                    work[rows, cols] -= dot3(left, (prev_hi[:, cols], prev_lo[:, cols]), TN)
+
+            return carry
+
+        lax.fori_loop(k + 1, count, inner, 0)
         return carry
 
     lax.fori_loop(0, count, outer, 0)
@@ -488,12 +495,13 @@
             pltpu.VMEM((2 * slots, half, TILE), jnp.float32),
             pltpu.VMEM((slots, half, TILE), jnp.float32),
             pltpu.VMEM((n_col * slots, TILE, TILE), jnp.float32),
-            pltpu.VMEM((eliminated, eliminated), jnp.float32),
+            pltpu.VMEM((eliminated, eliminated + share), jnp.float32),
             pltpu.VMEM((n_row // 2, eliminated, share), jnp.float32),
             pltpu.VMEM((eliminated, share), jnp.float32),
             pltpu.VMEM((eliminated, share), jnp.float32),
             pltpu.VMEM((eliminated, share), jnp.float32),
-            pltpu.VMEM((eliminated, share), jnp.float32),
+            pltpu.VMEM((BLOCK, eliminated + share), jnp.bfloat16),
+            pltpu.VMEM((BLOCK, eliminated + share), jnp.bfloat16),
             dma((2, slots)),
             dma((2, slots)),
             dma((2, slots)),

time: 344 us -> 318 us (0.924)
  Pallas kernels: 327 us -> 299 us
    pallas_call x1, Pallas kernels: 221 us -> 198 us  [front_gram(): pl.pallas_call(functools.partial(front_kernel, n_front, n_col, cap), out_...]
    pallas_call x1, Pallas kernels: 106 us -> 101 us  [tail(): pl.pallas_call(functools.partial(tail_kernel, n_row, n_col), out_shape=ja...]
where the time goes in v2:
time: 318 us; the launch traced here: 316 us
  Pallas kernels  299 us (94%)
  other arithmetic  13.1 us (4%)
  local copies, waits for them, and re-layouts  3.35 us (1%)
    pallas_call x1, Pallas kernels, front_gram(): pl.pallas_call(functools.partial(front_kernel, n_front, n_col, cap), out_...  198 us
    pallas_call x1, Pallas kernels, tail(): pl.pallas_call(functools.partial(tail_kernel, n_row, n_col), out_shape=ja...  101 us
    scatter x1, other arithmetic, body(): jnp.zeros((n_front * capacity, half_cols), jnp.float32).at[position]  8.82 us

profile of v2, /device:TPU:23, one launch (start us, length us, event | category | flops | bytes accessed | tf_op | source)
XLA Modules:
  0.0 315.7 jit_solution(11844163620469759059)
XLA Ops:
  0.0 0.7 broadcast_multiply_fusion
  0.7 0.7 fusion.10
  1.4 1.2 reduce-window.6
  2.6 0.2 slice_reduce_fusion
  2.8 0.2 reduce-window.9
  3.0 0.1 add_bitcast_fusion
  3.1 0.7 fusion.9
  3.8 0.7 compare_select_fusion
  4.5 8.8 %scatter_custom_fusion.send = f32[1024,2048]{1,0:T(8,128)} fusion(s32[512]{0:T(512)S(1)} %bitcast.32, f32[512,2048]{1,0:T(8,128)} %param.5, f32[]{:T(128)} %constant.14.clone.1, s32[2048]{0:T(1024)S(1)} %iota_add_fusion, s32[512]{0:T(512)S(1)} %broadcast_multiply_fusion), kind=kCustom, calls=%fused_computation.1 | custom fusion | flops 2097152 | bytes 12594176 | tf_op jit(solution)/shard_map/scatter | solution.py:540
  13.3 198.4 %shard_map.46 = (f32[1024,2048]{1,0:T(8,128)}, f32[5,256,256]{2,1,0:T(8,128)}) custom-call(f32[384,2048]{1,0:T(8,128)} %bitcast.27, f32[1024,2048]{1,0:T(8,128)} %scatter_custom_fusion.send), custom_call_target="tpu_custom_call" | custom-call | tf_op jit(solution)/shard_map/pallas_call | solution.py:201
  211.7 100.9 %shard_map.47 = f32[256,2048]{1,0:T(8,128)} custom-call(f32[1024,2048]{1,0:T(8,128)} %get-tuple-element.7.prod, f32[5,256,256]{2,1,0:T(8,128)} %get-tuple-element.8.square), custom_call_target="tpu_custom_call" | custom-call | tf_op jit(solution)/shard_map/pallas_call | solution.py:489
  312.6 3.1 copy.8
  (1 shorter events, 0.0 us)

commit v3 on v2

--- a/solution.py
+++ b/solution.py
@@ -9,6 +9,7 @@
 PANEL_COLUMNS = 512
 PANEL_COUNT = 2
 STAIR_BLK = 128
+STAIRS = 8
 BLOCK = 128
 HALF = 64
 TILE = 256
@@ -24,14 +25,24 @@
     return hi, (x - hi.astype(jnp.float32)).astype(jnp.bfloat16)
 
 
+def dot(a, b, dims):
+    return lax.dot_general(a, b, dims, preferred_element_type=jnp.float32)
+
+
 def dot3(a, b, dims):
     a_hi, a_lo = a
     b_hi, b_lo = b
-
-    def dot(x, y):
-        return lax.dot_general(x, y, dims, preferred_element_type=jnp.float32)
-
-    return dot(a_lo, b_hi) + dot(a_hi, b_lo) + dot(a_hi, b_hi)
+    return dot(a_lo, b_hi, dims) + dot(a_hi, b_lo, dims) + dot(a_hi, b_hi, dims)
+
+
+def left_of(x, axis=0):
+    hi, lo = split(x)
+    return jnp.concatenate([lo, hi, hi], axis)
+
+
+def right_of(x):
+    hi, lo = split(x)
+    return jnp.concatenate([hi, lo, hi], 0)
 
 
 def shift_order(n):
@@ -63,8 +74,8 @@
 
 
 def front_kernel(
-    n_front, n_col, cap, own, send, prod, square,
-    rows, pan, hi, lo, zs, zr, ys, yr, here_sem,
+    n_front, n_col, cap, codes, own, child, prod, square,
+    rows, pan, lhs, source, parcel, zs, zr, ys, yr, here_sem,
 ):
     f = lax.axis_index("front")
     c = lax.axis_index("col")
@@ -76,6 +87,12 @@
     first = n_own + cap
     count = (n_front - 1) * per
 
+    local = [
+        pltpu.make_async_copy(child, source, here_sem.at[0]),
+        pltpu.make_async_copy(own, rows.at[pl.ds(0, n_own)], here_sem.at[1]),
+    ]
+    for copy in local:
+        copy.start()
     barrier = pltpu.get_barrier_semaphore()
     for s in range(1, n_front):
         pl.semaphore_signal(
@@ -85,28 +102,16 @@
         pl.semaphore_signal(
             barrier, inc=1, device_id={"col": (c + s) % n_col}, device_id_type=MESH
         )
-
-    local = [
-        pltpu.make_async_copy(own, rows.at[pl.ds(0, n_own)], here_sem.at[0]),
-        pltpu.make_async_copy(
-            send.at[pl.ds(0, cap)], rows.at[pl.ds(n_own, cap)], here_sem.at[1]
-        ),
-    ]
-    for copy in local:
-        copy.start()
     pl.semaphore_wait(barrier, n_front - 1 + n_col - 1)
 
     def z_copy(j, target):
         return remote(
-            send.at[pl.ds(pl.multiple_of(cap + j * piece, piece), piece)],
+            parcel.at[pl.ds(pl.multiple_of(j * piece, piece), piece)],
             rows.at[pl.ds(pl.multiple_of(first + j * piece, piece), piece)],
             zs.at[j],
             zr.at[j],
             {"front": target},
         )
-
-    for j in range(count):
-        z_copy(j, (f + order[1 + j // per]) % n_front).start()
 
     groups = list(range(n_front - 1))
     late = sorted(groups, key=lambda q: (-min(order[1 + q], n_front - order[1 + q]), -q))
@@ -120,6 +125,28 @@
             {"col": other},
         )
 
+    columns = c * width + lax.broadcasted_iota(jnp.int32, (1, width), 1)
+
+    def pack(into, start, code_start, size):
+        def one(i, carry):
+            code = codes[code_start + i] - 1
+            row = source[pl.ds(jnp.maximum(code, 0) // STAIRS, 1), :]
+            edge = jnp.where(code < 0, n_col * width, code % STAIRS * STAIR_BLK)
+            into[pl.ds(start + i, 1), :] = jnp.where(columns >= edge, row, 0.0)
+            return carry
+
+        lax.fori_loop(0, size, one, 0, unroll=4)
+
+    local[0].wait()
+
+    def post(j, carry):
+        pack(parcel, j * piece, cap + j * piece, piece)
+        z_copy(j, (f + pick(j // per, order[1:])) % n_front).start()
+        return carry
+
+    lax.fori_loop(0, count, post, 0)
+    pack(rows, n_own, 0, cap)
+
     prod[...] = jnp.zeros_like(prod)
     square[...] = jnp.zeros_like(square)
     lists = square_tiles(eliminated, n_col)
@@ -129,37 +156,33 @@
         def _():
             for other in range(1, n_col):
                 y_copy(slot, start, size, other).start()
-            h, l = split(rows[pl.ds(start, size), pl.ds(0, eliminated)])
-            hi[pl.ds(0, size)] = h
-            lo[pl.ds(0, size)] = l
+            lhs[pl.ds(0, 3 * size)] = left_of(rows[pl.ds(start, size), pl.ds(0, eliminated)])
 
         @pl.when(c > 0)
         def _():
             y_copy(slot, start, size, 1).wait_recv()
-            h, l = split(pan[pl.ds(start, size)])
-            hi[pl.ds(0, size)] = h
-            lo[pl.ds(0, size)] = l
-
-        def lhs(i):
-            at = pl.ds(pl.multiple_of(i * TILE, TILE), TILE)
-            return hi[pl.ds(0, size), at], lo[pl.ds(0, size), at]
+            lhs[pl.ds(0, 3 * size)] = left_of(pan[pl.ds(start, size)])
 
         def column(n, carry):
             at = pl.ds(pl.multiple_of(n * TILE, TILE), TILE)
-            rhs = split(rows[pl.ds(start, size), at])
+            rhs = right_of(rows[pl.ds(start, size), at])
             for i in range(eliminated // TILE):
-                prod[pl.ds(i * TILE, TILE), at] += dot3(lhs(i), rhs, TN)
+                tile = pl.ds(i * TILE, TILE)
+                prod[tile, at] += dot(lhs[pl.ds(0, 3 * size), tile], rhs, TN)
             return carry
 
         lax.fori_loop(0, width // TILE, column, 0)
         for j in range(len(lists[0])):
             a = pick(c, [t[min(j, len(t) - 1)][0] for t in lists])
             b = pick(c, [t[min(j, len(t) - 1)][1] for t in lists])
-            square[j] += dot3(lhs(a), lhs(b), TN)
-
-    local[0].wait()
+            row = pl.ds(pl.multiple_of(a * TILE, TILE), TILE)
+            col = pl.ds(pl.multiple_of(b * TILE, TILE), TILE)
+            lo, hi = lhs[pl.ds(0, size), col], lhs[pl.ds(size, size), col]
+            rhs = jnp.concatenate([hi, lo, hi], 0)
+            square[j] += dot(lhs[pl.ds(0, 3 * size), row], rhs, TN)
+
+    local[1].wait()
     consume(0, 0, n_own)
-    local[1].wait()
     consume(1, n_own, cap)
 
     def arrived(i, carry):
@@ -191,7 +214,7 @@
     lax.fori_loop(0, count, left, 0)
 
 
-def front_gram(own, send, n_front, n_col, cap, eliminated):
+def front_gram(codes, own, child, n_front, n_col, cap, eliminated):
     n_own, width = own.shape
     total = n_own + n_front * cap
     piece = min(PIECE, cap)
@@ -204,13 +227,14 @@
             jax.ShapeDtypeStruct((eliminated, width), jnp.float32),
             jax.ShapeDtypeStruct((slots, TILE, TILE), jnp.float32),
         ),
-        in_specs=[pl.BlockSpec(memory_space=pl.ANY)] * 2,
+        in_specs=[pl.BlockSpec(memory_space=pltpu.SMEM)] + [pl.BlockSpec(memory_space=pl.ANY)] * 2,
         out_specs=(pl.BlockSpec(memory_space=pltpu.VMEM),) * 2,
         scratch_shapes=[
             pltpu.VMEM((total, width), jnp.float32),
             pltpu.VMEM((total, eliminated), jnp.float32),
-            pltpu.VMEM((most, eliminated), jnp.bfloat16),
-            pltpu.VMEM((most, eliminated), jnp.bfloat16),
+            pltpu.VMEM((3 * most, eliminated), jnp.bfloat16),
+            pltpu.VMEM(child.shape, jnp.float32),
+            pltpu.VMEM((count * piece, width), jnp.float32),
             pltpu.SemaphoreType.DMA((count,)),
             pltpu.SemaphoreType.DMA((count,)),
             pltpu.SemaphoreType.DMA((count + 2, n_col)),
@@ -220,7 +244,7 @@
         compiler_params=pltpu.CompilerParams(
             collective_id=0, has_side_effects=True, vmem_limit_bytes=60 << 20
         ),
-    )(own, send)
+    )(codes, own, child)
 
 
 def small_inverse(block):
@@ -289,7 +313,7 @@
 def tail_kernel(
     n_row, n_col, prod, square, out,
     part, other, whole_sq, work, near, leave, far, ready,
-    prev_hi, prev_lo,
+    prev,
     s1, s2, s3, s4, s5, r1, r2, ro_s, ro_r,
 ):
     r = lax.axis_index("row")
@@ -427,25 +451,26 @@
 
     def outer(k, carry):
         at = pl.ds(pl.multiple_of(k * BLOCK, BLOCK), BLOCK)
-        scale = split(block_inverse(work[at, at]))
+        scale = left_of(block_inverse(work[at, at]), 1)
         far_copy(k).wait_recv()
-        result = dot3(scale, split(work[at, eliminated:] + far[at]), NN)
+        result = dot(scale, right_of(work[at, eliminated:] + far[at]), NN)
         ready[at] = result
-        prev_hi[:, eliminated:], prev_lo[:, eliminated:] = split(result)
-        top = dot3(scale, split(work[at, :eliminated]), NN)
+        prev[:, eliminated:] = right_of(result)
+        top = dot(scale, right_of(work[at, :eliminated]), NN)
         top = jnp.where(lanes >= (k + 1) * BLOCK, top, 0.0)
-        prev_hi[:, :eliminated], prev_lo[:, :eliminated] = split(top)
+        prev[:, :eliminated] = right_of(top)
         deliver(k)
 
         def inner(j, carry):
             rows = pl.ds(pl.multiple_of(j * BLOCK, BLOCK), BLOCK)
-            left = prev_hi[:, rows], prev_lo[:, rows]
+            hi, lo = prev[:BLOCK, rows], prev[BLOCK : 2 * BLOCK, rows]
+            left = jnp.concatenate([lo, hi, hi], 0)
             for start in range(0, total, CHUNK):
                 cols = slice(start, min(total, start + CHUNK))
 
                 @pl.when(j * BLOCK < cols.stop)
                 def _():
-                    work[rows, cols] -= dot3(left, (prev_hi[:, cols], prev_lo[:, cols]), TN)
+                    work[rows, cols] -= dot(left, prev[:, cols], TN)
 
             return carry
 
@@ -500,8 +525,7 @@
             pltpu.VMEM((eliminated, share), jnp.float32),
             pltpu.VMEM((eliminated, share), jnp.float32),
             pltpu.VMEM((eliminated, share), jnp.float32),
-            pltpu.VMEM((BLOCK, eliminated + share), jnp.bfloat16),
-            pltpu.VMEM((BLOCK, eliminated + share), jnp.bfloat16),
+            pltpu.VMEM((3 * BLOCK, eliminated + share), jnp.bfloat16),
             dma((2, slots)),
             dma((2, slots)),
             dma((2, slots)),
@@ -522,24 +546,24 @@
     n_front = lax.axis_size("front")
     n_row = lax.axis_size("row")
     n_col = lax.axis_size("col")
-    source_rows, half_cols = child_rows.shape
+    source_rows = child_rows.shape[0]
     capacity = max(2, 2 * source_rows // n_front)
-    col_index = lax.axis_index("col")
-    global_cols = col_index * half_cols + lax.broadcasted_iota(
-        jnp.int32, (source_rows, half_cols), 1
-    )
-    masked_rows = jnp.where(global_cols >= (child_stair * STAIR_BLK)[:, None], child_rows, 0.0)
     targets = child_dest[:, 0]
-    onehot = (targets[:, None] == jnp.arange(n_front, dtype=jnp.int32)[None, :]).astype(jnp.int32)
-    slot = jnp.sum((jnp.cumsum(onehot, axis=0) - onehot) * onehot, axis=1)
+    index = lax.iota(jnp.int32, source_rows)
+    ahead = (targets[None, :] == targets[:, None]) & (index[None, :] < index[:, None])
+    slot = jnp.sum(ahead.astype(jnp.int32), axis=1)
     shift = (targets - lax.axis_index("front")) % n_front
     rank = jnp.zeros_like(shift)
     for place, s in enumerate(shift_order(n_front)):
         rank = jnp.where(shift == s, place + 1, rank)
     position = rank * capacity + slot
-    send = jnp.zeros((n_front * capacity, half_cols), jnp.float32).at[position].set(masked_rows)
+    code = index * STAIRS + child_stair + 1
+    places = lax.iota(jnp.int32, n_front * capacity)
+    codes = jnp.sum(jnp.where(position[None, :] == places[:, None], code[None, :], 0), axis=1)
     eliminated = PANEL_COUNT * PANEL_COLUMNS
-    prod, square = front_gram(own_rows[0], send, n_front, n_col, capacity, eliminated)
+    prod, square = front_gram(
+        codes, own_rows[0], child_rows, n_front, n_col, capacity, eliminated
+    )
     return tail(prod, square, n_row, n_col)[None]
 
 

time: 318 us -> 303 us (0.953)
  other arithmetic: 13.1 us -> 2.6 us
  Pallas kernels: 299 us -> 295 us
    scatter x1 -> x0, other arithmetic: 8.82 us -> none  [body(): jnp.zeros((n_front * capacity, half_cols), jnp.float32).at[position]]
where the time goes in v3:
time: 303 us; the launch traced here: 301 us
  Pallas kernels  295 us (97%)
  local copies, waits for them, and re-layouts  3.14 us (1%)
    pallas_call x1, Pallas kernels, front_gram(): pl.pallas_call(functools.partial(front_kernel, n_front, n_col, cap), out_...  197 us
    pallas_call x1, Pallas kernels, tail(): pl.pallas_call(functools.partial(tail_kernel, n_row, n_col), out_shape=ja...  98 us

profile of v3, /device:TPU:23, one launch (start us, length us, event | category | flops | bytes accessed | tf_op | source)
XLA Modules:
  0.0 301.1 jit_solution(5861801493749237498)
XLA Ops:
  0.0 1.0 convert_reduce_fusion
  1.0 0.7 add_add_fusion
  1.7 0.9 select_reduce_fusion.codes
  2.6 197.4 %shard_map.46 = (f32[1024,2048]{1,0:T(8,128)}, f32[5,256,256]{2,1,0:T(8,128)}) custom-call(s32[1024]{0:T(1024)} %select_reduce_fusion.codes, f32[384,2048]{1,0:T(8,128)} %bitcast.4, f32[512,2048]{1,0:T(8,128)} %child.1), custom_call_target="tpu_custom_call" | custom-call | tf_op jit(solution)/shard_map/pallas_call | solution.py:224
  200.0 98.0 %shard_map.47 = f32[256,2048]{1,0:T(8,128)} custom-call(f32[1024,2048]{1,0:T(8,128)} %get-tuple-element.7.prod, f32[5,256,256]{2,1,0:T(8,128)} %get-tuple-element.8.square), custom_call_target="tpu_custom_call" | custom-call | tf_op jit(solution)/shard_map/pallas_call | solution.py:514
  298.0 3.1 %copy.6 = f32[1,256,2048]{2,1,0:T(8,128)} copy(f32[1,256,2048]{2,1,0:T(8,128)} %bitcast.3) | data formatting | bytes 4194304

commit v4 on v3

v4 whole, which is shorter than its diff:
```python
import functools
import jax
import jax.numpy as jnp
from jax import lax
from jax.experimental import pallas as pl
from jax.experimental.pallas import tpu as pltpu
from jax.sharding import PartitionSpec as P

PANEL_COLUMNS = 512
PANEL_COUNT = 2
STAIR_BLK = 128
STAIRS = 8
BLOCK = 128
HALF = 64
TILE = 256
PIECE = 64
LATE = 2
CHUNK = 512
TN = (((0,), (0,)), ((), ()))
NN = (((1,), (0,)), ((), ()))
MESH = pl.DeviceIdType.MESH


def split(x):
    hi = x.astype(jnp.bfloat16)
    return hi, (x - hi.astype(jnp.float32)).astype(jnp.bfloat16)


def dot(a, b, dims):
    return lax.dot_general(a, b, dims, preferred_element_type=jnp.float32)


def dot3(a, b, dims):
    a_hi, a_lo = a
    b_hi, b_lo = b
    return dot(a_lo, b_hi, dims) + dot(a_hi, b_lo, dims) + dot(a_hi, b_hi, dims)


def left_of(x, axis=0):
    hi, lo = split(x)
    return jnp.concatenate([lo, hi, hi], axis)


def right_of(x):
    hi, lo = split(x)
    return jnp.concatenate([hi, lo, hi], 0)


def shift_order(n):
    return sorted(range(1, n), key=lambda s: (-min(s, n - s), s))


def square_tiles(eliminated, n_col):
    tiles = eliminated // TILE
    packed = [(i, k) for i in range(tiles) for k in range(i, tiles)]
    return [packed[c::n_col] for c in range(n_col)]


def pick(col, values):
    out = values[0]
    for c in range(1, len(values)):
        out = jnp.where(col == c, values[c], out)
    return out


def remote(src, dst, send_sem, recv_sem, device):
    return pltpu.make_async_remote_copy(
        src_ref=src,
        dst_ref=dst,
        send_sem=send_sem,
        recv_sem=recv_sem,
        device_id=device,
        device_id_type=MESH,
    )


def front_kernel(
    n_front, n_row, n_col, cap, codes, own, child, out,
    prod, square, rows, pan, lhs, source, parcel,
    part, other, whole_sq, work, near, far, prev, late_pan,
    zs, zr, ys, yr, here_sem,
    s1, s2, s3, s4, s5, r1, r2, ro_s, ro_r, x_late, own_late, far_late,
):
    f = lax.axis_index("front")
    r = lax.axis_index("row")
    c = lax.axis_index("col")
    n_own, width = own.shape
    eliminated = pan.shape[1]
    order = [0] + shift_order(n_front)
    piece = min(PIECE, cap)
    per = cap // piece
    first = n_own + cap
    count = (n_front - 1) * per

    local = [
        pltpu.make_async_copy(child, source, here_sem.at[0]),
        pltpu.make_async_copy(own, rows.at[pl.ds(0, n_own)], here_sem.at[1]),
    ]
    for copy in local:
        copy.start()
    barrier = pltpu.get_barrier_semaphore()
    for s in range(1, n_front):
        pl.semaphore_signal(
            barrier, inc=1, device_id={"front": (f + s) % n_front}, device_id_type=MESH
        )
    for s in range(1, n_row):
        pl.semaphore_signal(
            barrier, inc=1, device_id={"row": (r + s) % n_row}, device_id_type=MESH
        )
    for s in range(1, n_col):
        pl.semaphore_signal(
            barrier, inc=1, device_id={"col": (c + s) % n_col}, device_id_type=MESH
        )
    pl.semaphore_wait(barrier, n_front + n_row + n_col - 3)

    def z_copy(j, target):
        return remote(
            parcel.at[pl.ds(pl.multiple_of(j * piece, piece), piece)],
            rows.at[pl.ds(pl.multiple_of(first + j * piece, piece), piece)],
            zs.at[j],
            zr.at[j],
            {"front": target},
        )

    groups = list(range(n_front - 1))
    even = sorted(groups, key=lambda q: (-min(order[1 + q], n_front - order[1 + q]), -q))

    def y_copy(slot, start, size, other):
        return remote(
            rows.at[pl.ds(start, size), pl.ds(0, eliminated)],
            pan.at[pl.ds(start, size)],
            ys.at[slot, other],
            yr.at[slot],
            {"col": other},
        )

    columns = c * width + lax.broadcasted_iota(jnp.int32, (1, width), 1)

    def pack(into, start, code_start, size):
        def one(i, carry):
            code = codes[code_start + i] - 1
            row = source[pl.ds(jnp.maximum(code, 0) // STAIRS, 1), :]
            edge = jnp.where(code < 0, n_col * width, code % STAIRS * STAIR_BLK)
            into[pl.ds(start + i, 1), :] = jnp.where(columns >= edge, row, 0.0)
            return carry

        lax.fori_loop(0, size, one, 0, unroll=4)

    local[0].wait()

    def post(j, carry):
        pack(parcel, j * piece, cap + j * piece, piece)
        z_copy(j, (f + pick(j // per, order[1:])) % n_front).start()
        return carry

    lax.fori_loop(0, count, post, 0)
    pack(rows, n_own, 0, cap)

    prod[...] = jnp.zeros_like(prod)
    square[...] = jnp.zeros_like(square)
    lists = square_tiles(eliminated, n_col)
    slots = len(lists[0])

    def panel(slot, start, size):
        @pl.when(c == 0)
        def _():
            for other in range(1, n_col):
                y_copy(slot, start, size, other).start()
            lhs[pl.ds(0, 3 * size)] = left_of(rows[pl.ds(start, size), pl.ds(0, eliminated)])

        @pl.when(c > 0)
        def _():
            y_copy(slot, start, size, 1).wait_recv()
            lhs[pl.ds(0, 3 * size)] = left_of(pan[pl.ds(start, size)])

    def products(start, size):
        def column(n, carry):
            at = pl.ds(pl.multiple_of(n * TILE, TILE), TILE)
            rhs = right_of(rows[pl.ds(start, size), at])
            for i in range(eliminated // TILE):
                tile = pl.ds(i * TILE, TILE)
                prod[tile, at] += dot(lhs[pl.ds(0, 3 * size), tile], rhs, TN)
            return carry

        lax.fori_loop(0, width // TILE, column, 0)

    def square_dot(a, b, size):
        row = pl.ds(pl.multiple_of(a * TILE, TILE), TILE)
        col = pl.ds(pl.multiple_of(b * TILE, TILE), TILE)
        lo, hi = lhs[pl.ds(0, size), col], lhs[pl.ds(size, size), col]
        return dot(lhs[pl.ds(0, 3 * size), row], jnp.concatenate([hi, lo, hi], 0), TN)

    def consume(slot, start, size):
        panel(slot, start, size)
        products(start, size)
        for j in range(slots):
            a = pick(c, [t[min(j, len(t) - 1)][0] for t in lists])
            b = pick(c, [t[min(j, len(t) - 1)][1] for t in lists])
            square[j] += square_dot(a, b, size)

    local[1].wait()
    consume(0, 0, n_own)
    consume(1, n_own, cap)

    def place(i):
        group = jnp.where(f % 2 == 1, i // per, pick(i // per, even))
        return group * per + i % per

    def arrived(i, carry):
        j = place(i)
        z_copy(j, f).wait_recv()
        consume(2 + j, pl.multiple_of(first + j * piece, piece), piece)
        return carry

    lax.fori_loop(0, count - LATE, arrived, 0)
    share = width // n_row
    low = r % 2
    high = r // 2
    mate = r + 1 - 2 * low
    across = r + 2 - 4 * high
    y = n_col - 1 - c
    steps = eliminated // BLOCK
    owner_rows = eliminated // n_row
    half = TILE // 2

    kept = pl.ds(pl.multiple_of(low * half, half), half)
    given = pl.ds(pl.multiple_of((1 - low) * half, half), half)

    def core_copy(j):
        return remote(square.at[j, given], part.at[j], s1.at[0, j], s1.at[1, j], {"row": mate})

    def x_copy(j):
        return remote(part.at[slots + j], other.at[j], s2.at[0, j], s2.at[1, j], {"row": across})

    def flip_copy(j, col):
        tile = whole_sq.at[n_col * j + col, kept]
        return remote(tile, tile, s3.at[0, j], s3.at[1, j], {"col": y})

    def flip_recv(j):
        tile = whole_sq.at[n_col * j + y, kept]
        return remote(tile, tile, s3.at[0, j], s3.at[1, j], {"col": y})

    def mate_copy(j, col, sems):
        tile = whole_sq.at[n_col * j + col, kept]
        return remote(tile, tile, sems.at[0, j], sems.at[1, j], {"row": mate})

    def mate_recv(j, col, sems):
        tile = whole_sq.at[n_col * j + col, given]
        return remote(tile, tile, sems.at[0, j], sems.at[1, j], {"row": mate})

    def near_copy(q, k):
        at = pl.ds(pl.multiple_of(k * BLOCK, BLOCK), BLOCK)
        cols = pl.ds(pl.multiple_of((2 * q + 1 - low) * share, share), share)
        return remote(prod.at[at, cols], near.at[q, at], r1.at[0, q, k], r1.at[1, q, k], {"row": mate})

    theirs = pl.ds(pl.multiple_of((2 * (1 - high) + low) * share, share), share)
    ours = pl.ds(pl.multiple_of((2 * high + low) * share, share), share)

    def far_copy(k):
        at = pl.ds(pl.multiple_of(k * BLOCK, BLOCK), BLOCK)
        return remote(prod.at[at, theirs], far.at[at], r2.at[0, k], r2.at[1, k], {"row": across})

    def late_start(h):
        return pl.multiple_of(first + place(count - LATE + h) * piece, piece)

    def spread(h, source, device, sems):
        return remote(
            source,
            late_pan.at[r, pl.ds(h * piece, piece)],
            sems.at[0, h],
            sems.at[1, h],
            {"row": device},
        )

    def relay(h):
        there = late_pan.at[across, pl.ds(h * piece, piece)]
        return remote(there, there, far_late.at[0, h], far_late.at[1, h], {"row": mate})

    def received(h, source, sems):
        there = late_pan.at[source, pl.ds(h * piece, piece)]
        return remote(there, there, sems.at[0, h], sems.at[1, h], {"row": mate})

    def take(h):
        start = late_start(h)
        j = place(count - LATE + h)
        z_copy(j, f).wait_recv()
        panel(2 + j, start, piece)
        mine = pl.ds(h * piece, piece)

        @pl.when(c == 0)
        def _():
            there = rows.at[pl.ds(start, piece), pl.ds(0, eliminated)]
            spread(h, there, across, x_late).start()
            spread(h, there, mate, own_late).start()
            late_pan[r, mine] = rows[pl.ds(start, piece), pl.ds(0, eliminated)]

        @pl.when(c > 0)
        def _():
            there = pan.at[pl.ds(start, piece)]
            spread(h, there, across, x_late).start()
            spread(h, there, mate, own_late).start()
            late_pan[r, mine] = pan[pl.ds(start, piece)]

        products(start, piece)

    def late_square(h, add):
        received(h, mate, own_late).wait_recv()
        received(h, n_row - 1 - r, far_late).wait_recv()
        size = n_row * piece
        for q in range(n_row):
            hi, lo = split(late_pan[q, pl.ds(h * piece, piece)])
            lhs[pl.ds(q * piece, piece)] = lo
            lhs[pl.ds(size + q * piece, piece)] = hi
            lhs[pl.ds(2 * size + q * piece, piece)] = hi
        for col in range(n_col):
            for j, (a, b) in enumerate(lists[col]):
                tile = slice(a * TILE, (a + 1) * TILE), slice(b * TILE, (b + 1) * TILE)
                value = square_dot(a, b, size)
                if add:
                    value = value + work[tile]
                if h == LATE - 1:
                    value = value + whole_sq[n_col * j + col]
                work[tile] = value

    for j in range(slots):
        core_copy(j).start()
    for j in range(slots):
        core_copy(j).wait_recv()
        part[slots + j] = square[j, kept] + part[j]
        x_copy(j).start()
    for h in range(LATE - 1):
        take(h)
        if h == 0:
            for j in range(slots):
                x_copy(j).wait_recv()
                whole_sq[n_col * j + c, kept] = part[slots + j] + other[j]
                flip_copy(j, c).start()
                mate_copy(j, c, s4).start()
        received(h, across, x_late).wait_recv()
        relay(h).start()
        late_square(h, h > 0)
    take(LATE - 1)

    def hand(k, carry):
        for q in range(n_row // 2):
            near_copy(q, k).start()
        return carry

    lax.fori_loop(0, steps, hand, 0)
    for j in range(slots):
        flip_recv(j).wait_recv()
        mate_copy(j, y, s5).start()
    received(LATE - 1, across, x_late).wait_recv()
    relay(LATE - 1).start()
    for j in range(slots):
        mate_recv(j, c, s4).wait_recv()
        mate_recv(j, y, s5).wait_recv()
    late_square(LATE - 1, LATE > 1)

    def gather(k, carry):
        at = pl.ds(pl.multiple_of(k * BLOCK, BLOCK), BLOCK)
        for q in range(n_row // 2):
            near_copy(q, k).wait_recv()
        prod[at, theirs] += near[1 - high, at]
        far_copy(k).start()
        work[at, pl.ds(eliminated, share)] = prod[at, ours] + near[high, at]
        return carry

    lax.fori_loop(0, steps, gather, 0)

    def result_copy(k):
        at = pl.ds(pl.multiple_of(k * BLOCK, BLOCK), BLOCK)
        owner = k * BLOCK // owner_rows
        inside = pl.ds(pl.multiple_of(k * BLOCK % owner_rows, BLOCK), BLOCK)
        cols = pl.ds(pl.multiple_of(r * share, share), share)
        return remote(
            work.at[at, pl.ds(eliminated, share)],
            out.at[inside, cols],
            ro_s.at[k],
            ro_r.at[r, k % (owner_rows // BLOCK)],
            {"row": owner},
        )

    def result_recv(source, k):
        inside = pl.ds(k * BLOCK, BLOCK)
        cols = pl.ds(pl.multiple_of(source * share, share), share)
        return remote(
            work.at[inside, pl.ds(eliminated, share)],
            out.at[inside, cols],
            ro_s.at[k],
            ro_r.at[source, k],
            {"row": source},
        )

    def deliver(k):
        at = pl.ds(pl.multiple_of(k * BLOCK, BLOCK), BLOCK)
        owner = k * BLOCK // owner_rows

        @pl.when(owner == r)
        def _():
            inside = pl.ds(pl.multiple_of(k * BLOCK % owner_rows, BLOCK), BLOCK)
            out[inside, pl.ds(pl.multiple_of(r * share, share), share)] = work[at, eliminated:]

        @pl.when(owner != r)
        def _():
            result_copy(k).start()

    lanes = lax.broadcasted_iota(jnp.int32, (BLOCK, eliminated), 1)
    total = eliminated + share

    def outer(k, carry):
        at = pl.ds(pl.multiple_of(k * BLOCK, BLOCK), BLOCK)
        scale = left_of(block_inverse(work[at, at]), 1)
        far_copy(k).wait_recv()
        result = dot(scale, right_of(work[at, eliminated:] + far[at]), NN)
        work[at, eliminated:] = result
        prev[:, eliminated:] = right_of(result)
        top = dot(scale, right_of(work[at, :eliminated]), NN)
        top = jnp.where(lanes >= (k + 1) * BLOCK, top, 0.0)
        prev[:, :eliminated] = right_of(top)
        deliver(k)

        def inner(j, carry):
            rows = pl.ds(pl.multiple_of(j * BLOCK, BLOCK), BLOCK)
            hi, lo = prev[:BLOCK, rows], prev[BLOCK : 2 * BLOCK, rows]
            left = jnp.concatenate([lo, hi, hi], 0)
            for start in range(0, total, CHUNK):
                cols = slice(start, min(total, start + CHUNK))

                @pl.when(j * BLOCK < cols.stop)
                def _():
                    work[rows, cols] -= dot(left, prev[:, cols], TN)

            return carry

        lax.fori_loop(k + 1, steps, inner, 0)
        return carry

    lax.fori_loop(0, steps, outer, 0)

    for s in range(1, n_row):
        for k in range(owner_rows // BLOCK):
            result_recv((r + s) % n_row, k).wait_recv()

    def sent(k, carry):
        far_copy(k).wait_send()

        @pl.when(k * BLOCK // owner_rows != r)
        def _():
            result_copy(k).wait_send()

        return carry

    lax.fori_loop(0, steps, sent, 0)
    for j in range(slots):
        core_copy(j).wait_send()
        x_copy(j).wait_send()
        flip_copy(j, c).wait_send()
        mate_copy(j, c, s4).wait_send()
        mate_copy(j, y, s5).wait_send()
    for h in range(LATE):
        received(h, across, x_late).wait_send()
        received(h, mate, own_late).wait_send()
        relay(h).wait_send()

    def handed(k, carry):
        for q in range(n_row // 2):
            near_copy(q, k).wait_send()
        return carry

    lax.fori_loop(0, steps, handed, 0)

    @pl.when(c == 0)
    def _():
        for other in range(1, n_col):
            y_copy(0, 0, n_own, other).wait_send()
            y_copy(1, n_own, cap, other).wait_send()

            def sent(j, carry):
                start = pl.multiple_of(first + j * piece, piece)
                y_copy(2 + j, start, piece, other).wait_send()
                return carry

            lax.fori_loop(0, count, sent, 0)

    def left(j, carry):
        z_copy(j, f).wait_send()
        return carry

    lax.fori_loop(0, count, left, 0)


def small_inverse(block):
    lanes = lax.broadcasted_iota(jnp.int32, (HALF, HALF), 1)
    rows = lax.broadcasted_iota(jnp.int32, (HALF, HALF), 0)
    eye = (lanes == rows).astype(jnp.float32)
    both = jnp.concatenate([block, eye], 1)
    count = HALF // 8
    groups = [both[g * 8 : (g + 1) * 8] for g in range(count)]
    sub = lax.broadcasted_iota(jnp.int32, (8, 2 * HALF), 0)

    def column_of(g, j):
        return jnp.broadcast_to(groups[g][:, j : j + 1], (8, 2 * HALF))

    def row_of(x, s):
        return jnp.broadcast_to(x[s : s + 1], x.shape)

    for home in range(count):
        first = home * 8
        below = [[column_of(g, first + s) for s in range(8)] for g in range(home + 1, count)]
        columns = [column_of(home, first + s) for s in range(8)]
        solved = forward = groups[home]
        pivot = row_of(columns[0], 0)
        pivots = pivot
        for s in range(8):
            column = columns[s]
            inverse = 1.0 / pivot
            pivots = jnp.where(sub == s, pivot, pivots)
            forward = jnp.where(
                sub > s, forward - column * (row_of(forward, s) * inverse), forward
            )
            scaled = row_of(solved, s) * inverse
            solved = jnp.where(sub == s, scaled, solved - column * scaled)
            for t in range(s + 1, 8):
                row = row_of(columns[t], s)
                fresh = columns[t] - (column * row) * inverse
                if t == s + 1:
                    pivot = row_of(fresh, t)
                columns[t] = jnp.where(sub == s, row * inverse, fresh)
        groups[home] = forward * lax.rsqrt(pivots)
        spread = [row_of(solved, s) for s in range(8)]
        for g in range(home + 1, count):
            terms = [below[g - home - 1][s] * spread[s] for s in range(8)]
            while len(terms) > 1:
                terms = [terms[i] + terms[i + 1] for i in range(0, len(terms), 2)]
            groups[g] = groups[g] - terms[0]
    return jnp.concatenate(groups, 0)[:, HALF:]


def block_inverse(d):
    first = small_inverse(d[:HALF, :HALF])
    first_parts = split(first)
    r12 = dot3(first_parts, split(d[:HALF, HALF:]), NN)
    r12_parts = split(r12)
    second = small_inverse(d[HALF:, HALF:] - dot3(r12_parts, r12_parts, TN))
    corner = -dot3(split(second), split(dot3(r12_parts, first_parts, TN)), NN)
    return jnp.concatenate(
        [
            jnp.concatenate([first, jnp.zeros((HALF, HALF), jnp.float32)], 1),
            jnp.concatenate([corner, second], 1),
        ],
        0,
    )


def factor(codes, own, child, n_front, n_row, n_col, cap, eliminated):
    n_own, width = own.shape
    total = n_own + n_front * cap
    piece = min(PIECE, cap)
    count = (n_front - 1) * (cap // piece)
    slots = len(square_tiles(eliminated, n_col)[0])
    most = max(n_own, cap, n_row * piece)
    share = width // n_row
    steps = eliminated // BLOCK
    owner_rows = eliminated // n_row
    half = TILE // 2
    dma = pltpu.SemaphoreType.DMA
    f32 = jnp.float32
    return pl.pallas_call(
        functools.partial(front_kernel, n_front, n_row, n_col, cap),
        out_shape=jax.ShapeDtypeStruct((owner_rows, width), f32),
        in_specs=[pl.BlockSpec(memory_space=pltpu.SMEM)] + [pl.BlockSpec(memory_space=pl.ANY)] * 2,
        out_specs=pl.BlockSpec(memory_space=pltpu.VMEM),
        scratch_shapes=[
            pltpu.VMEM((eliminated, width), f32),
            pltpu.VMEM((slots, TILE, TILE), f32),
            pltpu.VMEM((total, width), f32),
            pltpu.VMEM((total, eliminated), f32),
            pltpu.VMEM((3 * most, eliminated), jnp.bfloat16),
            pltpu.VMEM(child.shape, f32),
            pltpu.VMEM((count * piece, width), f32),
            pltpu.VMEM((2 * slots, half, TILE), f32),
            pltpu.VMEM((slots, half, TILE), f32),
            pltpu.VMEM((n_col * slots, TILE, TILE), f32),
            pltpu.VMEM((eliminated, eliminated + share), f32),
            pltpu.VMEM((n_row // 2, eliminated, share), f32),
            pltpu.VMEM((eliminated, share), f32),
            pltpu.VMEM((3 * BLOCK, eliminated + share), jnp.bfloat16),
            pltpu.VMEM((n_row, LATE * piece, eliminated), f32),
            dma((count,)),
            dma((count,)),
            dma((count + 2, n_col)),
            dma((count + 2,)),
            dma((2,)),
            dma((2, slots)),
            dma((2, slots)),
            dma((2, slots)),
            dma((2, slots)),
            dma((2, slots)),
            dma((2, n_row // 2, steps)),
            dma((2, steps)),
            dma((steps,)),
            dma((n_row, owner_rows // BLOCK)),
            dma((2, LATE)),
            dma((2, LATE)),
            dma((2, LATE)),
        ],
        compiler_params=pltpu.CompilerParams(
            collective_id=0, has_side_effects=True, vmem_limit_bytes=67043328
        ),
    )(codes, own, child)


def body(own_rows, child_rows, child_dest, child_stair):
    n_front = lax.axis_size("front")
    n_row = lax.axis_size("row")
    n_col = lax.axis_size("col")
    source_rows = child_rows.shape[0]
    capacity = max(2, 2 * source_rows // n_front)
    targets = child_dest[:, 0]
    index = lax.iota(jnp.int32, source_rows)
    ahead = (targets[None, :] == targets[:, None]) & (index[None, :] < index[:, None])
    slot = jnp.sum(ahead.astype(jnp.int32), axis=1)
    shift = (targets - lax.axis_index("front")) % n_front
    rank = jnp.zeros_like(shift)
    for place, s in enumerate(shift_order(n_front)):
        rank = jnp.where(shift == s, place + 1, rank)
    position = rank * capacity + slot
    code = index * STAIRS + child_stair + 1
    places = lax.iota(jnp.int32, n_front * capacity)
    codes = jnp.sum(jnp.where(position[None, :] == places[:, None], code[None, :], 0), axis=1)
    eliminated = PANEL_COUNT * PANEL_COLUMNS
    result = factor(
        codes, own_rows[0], child_rows, n_front, n_row, n_col, capacity, eliminated
    )
    return result[None]


def solution(mesh):
    placed = (
        P("front", "row", "col"),
        P(("front", "row"), "col"),
        P(("front", "row"), None),
        P(("front", "row")),
    )
    return jax.shard_map(
        body, mesh=mesh, in_specs=placed, out_specs=P("front", "row", "col"), check_vma=False
    )
```

time: 303 us -> 303 us (level)
  the two profiles are of different devices: /device:TPU:23 before, /device:TPU:7 now
where the time goes in v4:
time: 303 us
  Pallas kernels  297 us (98%)
  local copies, waits for them, and re-layouts  3.14 us (1%)
    pallas_call x1, Pallas kernels, factor(): pl.pallas_call(functools.partial(front_kernel, n_front, n_row, n_col, cap...  297 us

profile of v4, /device:TPU:7, one launch (start us, length us, event | category | flops | bytes accessed | tf_op | source)
XLA Modules:
  0.0 303.2 jit_solution(16190359376036492434)
XLA Ops:
  0.0 1.0 convert_reduce_fusion
  1.0 0.7 add_add_fusion
  1.7 0.9 select_reduce_fusion.codes
  2.6 297.5 %shard_map.46 = f32[256,2048]{1,0:T(8,128)} custom-call(s32[1024]{0:T(1024)} %select_reduce_fusion.codes, f32[384,2048]{1,0:T(8,128)} %bitcast.4, f32[512,2048]{1,0:T(8,128)} %child.1), custom_call_target="tpu_custom_call" | custom-call | tf_op jit(solution)/shard_map/pallas_call | solution.py:569
  300.1 3.1 %copy.6 = f32[1,256,2048]{2,1,0:T(8,128)} copy(f32[1,256,2048]{2,1,0:T(8,128)} %bitcast.3) | data formatting | bytes 4194304

commit v5 on v4

--- a/solution.py
+++ b/solution.py
@@ -48,6 +48,28 @@
 
 def shift_order(n):
     return sorted(range(1, n), key=lambda s: (-min(s, n - s), s))
+
+
+def send_order(f, n):
+    up, down = list(range(n - 1, f, -1)), list(range(f))
+    return down + up if 2 * f < n else up[::-1] + down
+
+
+def arrival(f, g, n):
+    place = send_order(f, n).index(g)
+    depth = min(f, n - 1 - f)
+    return place + (depth if place >= depth else 0)
+
+
+def group_tables(n):
+    group = {s: q for q, s in enumerate(shift_order(n))}
+    sends, takes = [], []
+    for f in range(n):
+        sends += [group[(g - f) % n] for g in send_order(f, n)]
+        sources = [g for g in range(n) if g != f]
+        sources.sort(key=lambda g: arrival(g, f, n))
+        takes += [group[(f - g) % n] for g in sources]
+    return sends, takes
 
 
 def square_tiles(eliminated, n_col):
@@ -122,8 +144,7 @@
             {"front": target},
         )
 
-    groups = list(range(n_front - 1))
-    even = sorted(groups, key=lambda q: (-min(order[1 + q], n_front - order[1 + q]), -q))
+    sends, takes = group_tables(n_front)
 
     def y_copy(slot, start, size, other):
         return remote(
@@ -148,7 +169,8 @@
 
     local[0].wait()
 
-    def post(j, carry):
+    def post(i, carry):
+        j = pick(f * (n_front - 1) + i // per, sends) * per + i % per
         pack(parcel, j * piece, cap + j * piece, piece)
         z_copy(j, (f + pick(j // per, order[1:])) % n_front).start()
         return carry
@@ -203,7 +225,7 @@
     consume(1, n_own, cap)
 
     def place(i):
-        group = jnp.where(f % 2 == 1, i // per, pick(i // per, even))
+        group = pick(f * (n_front - 1) + i // per, takes)
         return group * per + i % per
 
     def arrived(i, carry):

time: 303 us -> 294 us (0.970)
  the two profiles are of different devices: /device:TPU:7 before, /device:TPU:23 now
where the time goes in v5:
time: 294 us; the launch traced here: 292 us
  Pallas kernels  287 us (98%)
  local copies, waits for them, and re-layouts  3.14 us (1%)
    pallas_call x1, Pallas kernels, factor(): pl.pallas_call(functools.partial(front_kernel, n_front, n_row, n_col, cap...  287 us

profile of v5, /device:TPU:23, one launch (start us, length us, event | category | flops | bytes accessed | tf_op | source)
XLA Modules:
  0.0 292.3 jit_solution(3353255976843082394)
XLA Ops:
  0.0 1.0 convert_reduce_fusion
  1.0 0.7 add_add_fusion
  1.7 0.9 select_reduce_fusion.codes
  2.6 286.5 %shard_map.46 = f32[256,2048]{1,0:T(8,128)} custom-call(s32[1024]{0:T(1024)} %select_reduce_fusion.codes, f32[384,2048]{1,0:T(8,128)} %bitcast.4, f32[512,2048]{1,0:T(8,128)} %child.1), custom_call_target="tpu_custom_call" | custom-call | tf_op jit(solution)/shard_map/pallas_call | solution.py:591
  289.1 3.1 %copy.6 = f32[1,256,2048]{2,1,0:T(8,128)} copy(f32[1,256,2048]{2,1,0:T(8,128)} %bitcast.3) | data formatting | bytes 4194304

commit v6 on v5

--- a/solution.py
+++ b/solution.py
@@ -15,6 +15,7 @@
 TILE = 256
 PIECE = 64
 LATE = 2
+AHEAD = 2
 CHUNK = 512
 TN = (((0,), (0,)), ((), ()))
 NN = (((1,), (0,)), ((), ()))
@@ -180,6 +181,7 @@
 
     prod[...] = jnp.zeros_like(prod)
     square[...] = jnp.zeros_like(square)
+    work[:, eliminated:] = jnp.zeros((eliminated, work.shape[1] - eliminated), jnp.float32)
     lists = square_tiles(eliminated, n_col)
     slots = len(lists[0])
 
@@ -385,10 +387,10 @@
             near_copy(q, k).wait_recv()
         prod[at, theirs] += near[1 - high, at]
         far_copy(k).start()
-        work[at, pl.ds(eliminated, share)] = prod[at, ours] + near[high, at]
-        return carry
-
-    lax.fori_loop(0, steps, gather, 0)
+        work[at, pl.ds(eliminated, share)] += prod[at, ours] + near[high, at]
+        return carry
+
+    lax.fori_loop(0, AHEAD, gather, 0)
 
     def result_copy(k):
         at = pl.ds(pl.multiple_of(k * BLOCK, BLOCK), BLOCK)
@@ -432,6 +434,9 @@
 
     def outer(k, carry):
         at = pl.ds(pl.multiple_of(k * BLOCK, BLOCK), BLOCK)
+        lax.fori_loop(
+            jnp.minimum(AHEAD * (k + 1), steps), jnp.minimum(AHEAD * (k + 2), steps), gather, 0
+        )
         scale = left_of(block_inverse(work[at, at]), 1)
         far_copy(k).wait_recv()
         result = dot(scale, right_of(work[at, eliminated:] + far[at]), NN)

time: 294 us -> 294 us (level)
  no operation moved by 1% of the time
where the time goes in v6:
time: 294 us; the launch traced here: 293 us
  Pallas kernels  287 us (98%)
  local copies, waits for them, and re-layouts  3.14 us (1%)
    pallas_call x1, Pallas kernels, factor(): pl.pallas_call(functools.partial(front_kernel, n_front, n_row, n_col, cap...  287 us

profile of v6, /device:TPU:23, one launch (start us, length us, event | category | flops | bytes accessed | tf_op | source)
XLA Modules:
  0.0 292.6 jit_solution(7626828306931375262)
XLA Ops:
  0.0 1.0 convert_reduce_fusion
  1.0 0.7 add_add_fusion
  1.7 0.9 select_reduce_fusion.codes
  2.6 286.9 %shard_map.46 = f32[256,2048]{1,0:T(8,128)} custom-call(s32[1024]{0:T(1024)} %select_reduce_fusion.codes, f32[384,2048]{1,0:T(8,128)} %bitcast.4, f32[512,2048]{1,0:T(8,128)} %child.1), custom_call_target="tpu_custom_call" | custom-call | tf_op jit(solution)/shard_map/pallas_call | solution.py:596
  289.5 3.1 %copy.6 = f32[1,256,2048]{2,1,0:T(8,128)} copy(f32[1,256,2048]{2,1,0:T(8,128)} %bitcast.3) | data formatting | bytes 4194304

commit v7 on v6

--- a/solution.py
+++ b/solution.py
@@ -370,12 +370,12 @@
             near_copy(q, k).start()
         return carry
 
-    lax.fori_loop(0, steps, hand, 0)
     for j in range(slots):
         flip_recv(j).wait_recv()
         mate_copy(j, y, s5).start()
     received(LATE - 1, across, x_late).wait_recv()
     relay(LATE - 1).start()
+    lax.fori_loop(0, steps, hand, 0)
     for j in range(slots):
         mate_recv(j, c, s4).wait_recv()
         mate_recv(j, y, s5).wait_recv()

time: 294 us -> 290 us (0.986)
  Pallas kernels: 287 us -> 283 us
    pallas_call x1, Pallas kernels: 287 us -> 283 us  [factor(): pl.pallas_call(functools.partial(front_kernel, n_front, n_row, n_col, cap...]
where the time goes in v7:
time: 290 us; the launch traced here: 289 us
  Pallas kernels  283 us (98%)
  local copies, waits for them, and re-layouts  3.14 us (1%)
    pallas_call x1, Pallas kernels, factor(): pl.pallas_call(functools.partial(front_kernel, n_front, n_row, n_col, cap...  283 us

profile of v7, /device:TPU:23, one launch (start us, length us, event | category | flops | bytes accessed | tf_op | source)
XLA Modules:
  0.0 288.6 jit_solution(494352234142024717)
XLA Ops:
  0.0 1.0 convert_reduce_fusion
  1.0 0.7 add_add_fusion
  1.7 0.9 select_reduce_fusion.codes
  2.6 282.9 %shard_map.46 = f32[256,2048]{1,0:T(8,128)} custom-call(s32[1024]{0:T(1024)} %select_reduce_fusion.codes, f32[384,2048]{1,0:T(8,128)} %bitcast.4, f32[512,2048]{1,0:T(8,128)} %child.1), custom_call_target="tpu_custom_call" | custom-call | tf_op jit(solution)/shard_map/pallas_call | solution.py:596
  285.5 3.1 %copy.6 = f32[1,256,2048]{2,1,0:T(8,128)} copy(f32[1,256,2048]{2,1,0:T(8,128)} %bitcast.3) | data formatting | bytes 4194304
